TPU v7x, 32 devices: a whole 2x2x4 slice. The times are simulated.
32 devices in a mesh: section: 2 (over core), expert: 4 (over z), tensor: 4 (over y, x).
Axes of the slice: x: 2, y: 2, z: 4, core: 2. Of those that a mesh axis runs over, the one named last changes fastest.
Arguments:
- x_in: bfloat16 [2, 4096, 768], P(None, 'expert'), may hold values from -6 to 6
- cotangent: bfloat16 [2, 4096, 768], P(None, 'expert'), may hold values from -6 to 6
- attn_gain: bfloat16 [2, 768], P('section'), may hold values from 0.5 to 1.5
- ffn_gain: bfloat16 [2, 768], P('section'), may hold values from 0.5 to 1.5
- w_query: bfloat16 [2, 768, 768], P('section', None, 'tensor'), may hold values from -0.21875 to 0.21875
- w_key: bfloat16 [2, 768, 768], P('section', None, 'tensor'), may hold values from -0.21875 to 0.21875
- w_value: bfloat16 [2, 768, 768], P('section', None, 'tensor'), may hold values from -0.21875 to 0.21875
- w_out: bfloat16 [2, 768, 768], P('section', 'tensor'), may hold values from -2.140625 to 2.140625
- rel_bias: bfloat16 [2, 32, 12], P('section', None, 'tensor'), may hold values from -5 to 5
- w_router: bfloat16 [2, 768, 16], P('section'), may hold values from -0.21875 to 0.21875
- w_in: bfloat16 [2, 16, 768, 3072], P('section', 'expert', None, 'tensor'), may hold values from -0.21875 to 0.21875
- w_back: bfloat16 [2, 16, 3072, 768], P('section', 'expert', 'tensor'), may hold values from -2.46875 to 2.46875
- routes: int32 [2, 2, 4096, 1], P('section', None, 'expert'), may hold values from 0 to 15; in each aligned block of 1024 rows (0 to 1023, 1024 to 2047, ..., all dimensions but the last counted through in order) at most 96 rows name the same one
- keep_mask: int32 [2, 2, 4096], P('section', None, 'expert'), may hold values 0 or 1
Outputs:
- acts: bfloat16 [2, 2, 4096, 768], P('section', None, 'expert')
- input_grads: bfloat16 [2, 2, 4096, 768], P('section', None, 'expert')
- g_attn_gain: float32 [2, 768], P('section', 'expert')
- g_ffn_gain: float32 [2, 768], P('section', 'expert')
- g_query: float32 [2, 768, 768], P('section', 'expert', 'tensor')
- g_key: float32 [2, 768, 768], P('section', 'expert', 'tensor')
- g_value: float32 [2, 768, 768], P('section', 'expert', 'tensor')
- g_out: float32 [2, 768, 768], P('section', 'tensor', 'expert')
- g_rel: float32 [2, 32, 12], P('section', 'expert', 'tensor')
- g_router: float32 [2, 768, 16], P('section', 'expert')
- g_in: float32 [2, 16, 768, 3072], P('section', 'expert', None, 'tensor')
- g_back: float32 [2, 16, 3072, 768], P('section', 'expert', 'tensor')
Inputs may be any that keep to these rules, and one draw needn't show every extreme that they name: `routes`: in each aligned block of 1024 tokens (one index of the expert axis, one section and micro-batch), no expert is named more than 96 times, and some block reaches 96.
All inputs are finite; a program needn't handle non-finite values. No bound on the sum of `keep_mask` on one device may be relied on, other than what follows from the above.
Results may differ from a plain program's by a relative error of at most 0.04.
Values may be sent and summed in bfloat16 or wider, within the bound.
No kernel may reach another device: no remote copies, remote signals or barrier semaphores. Data moves between devices by JAX's collectives and lax.ppermute only.
A program may use at most 384 MiB of HBM per device.

v0:
```python
import jax
import jax.numpy as jnp
import numpy as np
from jax import lax
from jax.sharding import PartitionSpec as P

DH = 64
LENGTH = 512


EPSILON = 1e-06
HIGHEST = lax.Precision.HIGHEST


def from_behind(block, axis, distance):
    devices = range(lax.axis_size(axis))
    route = [(i - distance, i) for i in devices if i - distance in devices]
    return lax.ppermute(block, axis, route)


def relative_buckets(seq_length):
    bucket_list = []
    for offset in range(-(seq_length - 1), seq_length):
        bucket = 16 if offset > 0 else 0
        distance = abs(offset)
        if distance < 8:
            bucket = bucket + distance
        else:
            ladder = 0
            while ladder < 7 and distance**8 >= 2 ** (24 + 4 * (ladder + 1)):
                ladder = ladder + 1
            bucket = bucket + 8 + ladder
        bucket_list.append(bucket)
    return np.array(bucket_list, dtype=np.int32)


def offset_grid(seq_length):
    return (
        np.arange(seq_length)[None, :] - np.arange(seq_length)[:, None] + (seq_length - 1)
    ).astype(np.int32)


def root_mean(values):
    return lax.rsqrt(jnp.mean(values * values, axis=-1, keepdims=True) + EPSILON)


def smooth(values):
    return jax.nn.gelu(values, approximate=False)


def norm_back(grad, values, scale, gain):
    scaled = grad * gain
    values_grad = scale * scaled - values * (scale * scale * scale) * jnp.mean(
        scaled * values, axis=-1, keepdims=True
    )
    gain_grad = jnp.sum(grad * values * scale, axis=0)
    return (values_grad, gain_grad)


def layer_forward(layer_in, weights, bias, route_rows, keep_rows):
    attn_gain, ffn_gain, w_query, w_key, w_value, w_out, w_router, w_in, w_back = weights
    tok_rows, width = layer_in.shape
    head_cols = w_query.shape[1]
    heads = head_cols // DH
    groups = lax.axis_size("expert")
    sequences = tok_rows // LENGTH
    scale_one = root_mean(layer_in)
    normed = (layer_in * scale_one * attn_gain).astype(jnp.bfloat16)
    query = jnp.dot(normed, w_query, preferred_element_type=jnp.float32).astype(jnp.bfloat16)
    keys_own = jnp.dot(normed, w_key, preferred_element_type=jnp.float32).astype(jnp.bfloat16)
    values_own = jnp.dot(normed, w_value, preferred_element_type=jnp.float32).astype(jnp.bfloat16)
    query_heads = query.reshape(sequences, LENGTH, heads, DH)
    keys_heads = keys_own.reshape(sequences, LENGTH, heads, DH)
    values_heads = values_own.reshape(sequences, LENGTH, heads, DH)
    scores = (
        jnp.einsum("sqhd,skhd->shqk", query_heads, keys_heads, preferred_element_type=jnp.float32)
        * 0.125
        + bias[None]
    )
    highest = jnp.max(scores, axis=-1, keepdims=True)
    raised = jnp.exp(scores - highest)
    total = jnp.sum(raised, axis=-1, keepdims=True)
    probs_low = (raised / total).astype(jnp.bfloat16)
    attended = jnp.einsum(
        "shqk,skhd->sqhd", probs_low, values_heads, preferred_element_type=jnp.float32
    )
    log_total = highest + jnp.log(total)
    mixed_low = attended.reshape(tok_rows, head_cols).astype(jnp.bfloat16)
    branch = lax.psum(
        jnp.dot(mixed_low, w_out, preferred_element_type=jnp.float32).astype(jnp.bfloat16), "tensor"
    ).astype(jnp.float32)
    middle = layer_in + branch
    scale_two = root_mean(middle)
    normed_two = (middle * scale_two * ffn_gain).astype(jnp.bfloat16)
    logits = jnp.dot(normed_two, w_router, preferred_element_type=jnp.float32)
    probs = jax.nn.softmax(logits, axis=-1)
    experts = w_router.shape[1]
    local = w_in.shape[0]
    capacity = 3 * tok_rows // (2 * experts)
    chosen_bool = route_rows[:, None] == jnp.arange(experts, dtype=jnp.int32)[None, :]
    chosen_int = chosen_bool.astype(jnp.int32)
    chosen = chosen_bool.astype(jnp.float32)
    gate = jnp.sum(probs * chosen, axis=-1)
    kept = keep_rows.astype(jnp.float32)
    running = jnp.cumsum(chosen_int, axis=0, dtype=jnp.int32)
    rank = jnp.sum((running - 1) * chosen_int, axis=-1, dtype=jnp.int32)
    slot = route_rows % local * (groups * capacity) + route_rows // local * capacity + rank
    slot = jnp.where(keep_rows > 0, slot, -1)
    placing = (jnp.arange(experts * capacity, dtype=jnp.int32)[:, None] == slot[None, :]).astype(
        jnp.bfloat16
    )
    outgoing = (
        jnp.dot(placing, normed_two, preferred_element_type=jnp.float32)
        .astype(jnp.bfloat16)
        .reshape(local, groups, capacity, width)
    )
    incoming = lax.all_to_all(outgoing, "expert", split_axis=1, concat_axis=1, tiled=True).reshape(
        local, groups * capacity, width
    )
    inner = jnp.einsum("end,edf->enf", incoming, w_in, preferred_element_type=jnp.float32)
    hidden = smooth(inner).astype(jnp.bfloat16)
    partial_out = jnp.einsum("enf,efd->end", hidden, w_back, preferred_element_type=jnp.float32)
    expert_out = lax.psum(partial_out, "tensor").astype(jnp.bfloat16)
    returned = lax.all_to_all(
        expert_out.reshape(local, groups, capacity, width),
        "expert",
        split_axis=1,
        concat_axis=1,
        tiled=True,
    ).reshape(experts * capacity, width)
    per_token = jnp.einsum("st,sd->td", placing, returned, preferred_element_type=jnp.float32)
    output = middle + (kept * gate)[:, None] * per_token
    saved = (
        layer_in,
        scale_one,
        normed,
        query,
        keys_own,
        values_own,
        log_total,
        mixed_low,
        middle,
        scale_two,
        normed_two,
        probs,
        chosen,
        gate,
        kept,
        placing,
        incoming,
        inner,
        per_token,
    )
    return (output, saved)


def layer_backward(saved, grad_out, weights, bias):
    attn_gain, ffn_gain, w_query, w_key, w_value, w_out, w_router, w_in, w_back = weights
    (
        layer_in,
        scale_one,
        normed,
        query,
        keys_own,
        values_own,
        log_total,
        mixed_low,
        middle,
        scale_two,
        normed_two,
        probs,
        chosen,
        gate,
        kept,
        placing,
        incoming,
        inner,
        per_token,
    ) = saved
    tok_rows, width = layer_in.shape
    head_cols = w_query.shape[1]
    heads = head_cols // DH
    groups = lax.axis_size("expert")
    sequences = tok_rows // LENGTH
    experts = w_router.shape[1]
    local = w_in.shape[0]
    capacity = 3 * tok_rows // (2 * experts)
    smooth_value, smooth_pull = jax.vjp(smooth, inner)
    hidden = smooth_value.astype(jnp.bfloat16)
    gated = ((kept * gate)[:, None] * grad_out).astype(jnp.bfloat16)
    gate_grad = kept * jnp.sum(grad_out * per_token, axis=-1)
    send_grad = (
        jnp.dot(placing, gated, preferred_element_type=jnp.float32)
        .astype(jnp.bfloat16)
        .reshape(local, groups, capacity, width)
    )
    expert_grad = lax.all_to_all(
        send_grad, "expert", split_axis=1, concat_axis=1, tiled=True
    ).reshape(local, groups * capacity, width)
    back_grad = jnp.einsum("enf,end->efd", hidden, expert_grad, preferred_element_type=jnp.float32)
    hidden_grad = jnp.einsum(
        "end,efd->enf", expert_grad, w_back, preferred_element_type=jnp.float32
    )
    inner_grad = smooth_pull(hidden_grad)[0].astype(jnp.bfloat16)
    in_grad = jnp.einsum("end,enf->edf", incoming, inner_grad, preferred_element_type=jnp.float32)
    input_part = jnp.einsum("enf,edf->end", inner_grad, w_in, preferred_element_type=jnp.float32)
    input_low = lax.psum(input_part.astype(jnp.bfloat16), "tensor")
    back_rows = lax.all_to_all(
        input_low.reshape(local, groups, capacity, width),
        "expert",
        split_axis=1,
        concat_axis=1,
        tiled=True,
    ).reshape(experts * capacity, width)
    normed_two_grad = jnp.einsum(
        "st,sd->td", placing, back_rows, preferred_element_type=jnp.float32
    )
    logit_grad = (probs * (chosen - gate[:, None]) * gate_grad[:, None]).astype(jnp.bfloat16)
    router_grad = jnp.einsum(
        "td,te->de", normed_two, logit_grad, preferred_element_type=jnp.float32
    )
    normed_two_grad = normed_two_grad + jnp.einsum(
        "te,de->td", logit_grad, w_router, preferred_element_type=jnp.float32
    )
    middle_part, ffn_grad = norm_back(normed_two_grad, middle, scale_two, ffn_gain)
    middle_grad = grad_out + middle_part
    branch_grad = middle_grad.astype(jnp.bfloat16)
    out_grad = jnp.einsum("tc,td->cd", mixed_low, branch_grad, preferred_element_type=jnp.float32)
    mixed_grad = jnp.einsum(
        "td,cd->tc", branch_grad, w_out, preferred_element_type=jnp.float32
    ).astype(jnp.bfloat16)
    grad_heads = mixed_grad.reshape(sequences, LENGTH, heads, DH)
    query_heads = query.reshape(sequences, LENGTH, heads, DH)
    keys_heads = keys_own.reshape(sequences, LENGTH, heads, DH)
    values_heads = values_own.reshape(sequences, LENGTH, heads, DH)
    scores = (
        jnp.einsum("sqhd,skhd->shqk", query_heads, keys_heads, preferred_element_type=jnp.float32)
        * 0.125
        + bias[None]
    )
    weights_now = jnp.exp(scores - log_total)
    low_weights = weights_now.astype(jnp.bfloat16)
    value_grad = jnp.einsum(
        "shqk,sqhd->skhd", low_weights, grad_heads, preferred_element_type=jnp.float32
    )
    weight_grad = jnp.einsum(
        "sqhd,skhd->shqk", grad_heads, values_heads, preferred_element_type=jnp.float32
    )
    weighted_sum = jnp.sum(weights_now * weight_grad, axis=-1, keepdims=True)
    score_grad = (weights_now * (weight_grad - weighted_sum)).astype(jnp.bfloat16)
    query_grad = (
        jnp.einsum("shqk,skhd->sqhd", score_grad, keys_heads, preferred_element_type=jnp.float32)
        * 0.125
    )
    key_grad = (
        jnp.einsum("shqk,sqhd->skhd", score_grad, query_heads, preferred_element_type=jnp.float32)
        * 0.125
    )
    bias_grad = jnp.sum(score_grad.astype(jnp.float32), axis=0)
    query_low = query_grad.reshape(tok_rows, head_cols).astype(jnp.bfloat16)
    key_low = key_grad.reshape(tok_rows, head_cols).astype(jnp.bfloat16)
    value_low = value_grad.reshape(tok_rows, head_cols).astype(jnp.bfloat16)
    query_wgrad = jnp.einsum("td,tc->dc", normed, query_low, preferred_element_type=jnp.float32)
    key_wgrad = jnp.einsum("td,tc->dc", normed, key_low, preferred_element_type=jnp.float32)
    value_wgrad = jnp.einsum("td,tc->dc", normed, value_low, preferred_element_type=jnp.float32)
    normed_part = jnp.einsum("tc,dc->td", query_low, w_query, preferred_element_type=jnp.float32)
    normed_part = normed_part + jnp.einsum(
        "tc,dc->td", key_low, w_key, preferred_element_type=jnp.float32
    )
    normed_part = normed_part + jnp.einsum(
        "tc,dc->td", value_low, w_value, preferred_element_type=jnp.float32
    )
    normed_grad = lax.psum(normed_part.astype(jnp.bfloat16), "tensor").astype(jnp.float32)
    layer_part, attn_grad = norm_back(normed_grad, layer_in, scale_one, attn_gain)
    layer_grad = middle_grad + layer_part
    parts = (
        attn_grad,
        ffn_grad,
        query_wgrad,
        key_wgrad,
        value_wgrad,
        out_grad,
        bias_grad,
        router_grad,
        in_grad,
        back_grad,
    )
    return (layer_grad, parts)


def body(
    x_in,
    cotangent,
    attn_gain,
    ffn_gain,
    w_query,
    w_key,
    w_value,
    w_out,
    rel_bias,
    w_router,
    w_in,
    w_back,
    routes,
    keep_mask,
):
    weights = (
        attn_gain[0].astype(jnp.float32),
        ffn_gain[0].astype(jnp.float32),
        w_query[0],
        w_key[0],
        w_value[0],
        w_out[0],
        w_router[0],
        w_in[0],
        w_back[0],
    )
    rel_local = rel_bias[0].astype(jnp.float32)
    buckets = rel_local.shape[0]
    table = jnp.asarray(relative_buckets(LENGTH))
    index_grid = jnp.asarray(offset_grid(LENGTH))
    picks = (table[:, None] == jnp.arange(buckets, dtype=jnp.int32)[None, :]).astype(jnp.float32)
    offsets = jnp.dot(picks, rel_local, precision=HIGHEST).T

    def make_bias(table_rows):
        return table_rows[:, index_grid]

    bias, bias_pull = jax.vjp(make_bias, offsets)
    section = lax.axis_index("section")
    first = section == 0
    micro = x_in.shape[0]
    tok_rows = x_in.shape[1]
    width = x_in.shape[2]
    received = jnp.zeros((tok_rows, width), jnp.bfloat16)
    acts = jnp.zeros((micro, tok_rows, width), jnp.bfloat16)
    saved_all = []
    for tick in range(micro + 1):
        batch = tick - section
        own = jnp.clip(batch, 0, micro - 1)
        valid = (batch >= 0) & (batch < micro)
        layer_in = jnp.where(first, x_in[min(tick, micro - 1)], received).astype(jnp.float32)
        route_rows = lax.dynamic_index_in_dim(routes[0], own, 0, keepdims=False)[:, 0]
        keep_rows = lax.dynamic_index_in_dim(keep_mask[0], own, 0, keepdims=False)
        output, saved = layer_forward(layer_in, weights, bias, route_rows, keep_rows)
        out_low = output.astype(jnp.bfloat16)
        current = lax.dynamic_index_in_dim(acts, own, 0, keepdims=False)
        acts = lax.dynamic_update_index_in_dim(acts, jnp.where(valid, out_low, current), own, 0)
        saved_all.append(saved)
        if tick < micro:
            received = from_behind(out_low, "section", 1)
    coming = jnp.zeros((tok_rows, width), jnp.bfloat16)
    input_grads = jnp.zeros((micro, tok_rows, width), jnp.bfloat16)
    totals = None
    for tick in range(micro + 1):
        batch = tick + section - 1
        own = jnp.clip(batch, 0, micro - 1)
        valid = (batch >= 0) & (batch < micro)
        early = saved_all[max(tick - 1, 0)]
        late = saved_all[min(tick + 1, micro)]
        saved = jax.tree.map(lambda left, right: jnp.where(first, left, right), early, late)
        grad_out = jnp.where(first, coming, cotangent[min(tick, micro - 1)]).astype(
            jnp.float32
        ) * valid.astype(jnp.float32)
        layer_grad, parts = layer_backward(saved, grad_out, weights, bias)
        grad_low = layer_grad.astype(jnp.bfloat16)
        current = lax.dynamic_index_in_dim(input_grads, own, 0, keepdims=False)
        input_grads = lax.dynamic_update_index_in_dim(
            input_grads, jnp.where(valid, grad_low, current), own, 0
        )
        totals = parts if totals is None else jax.tree.map(jnp.add, totals, parts)
        if tick < micro:
            coming = from_behind(grad_low, "section", -1)
    (
        attn_grad,
        ffn_grad,
        query_wgrad,
        key_wgrad,
        value_wgrad,
        out_grad,
        bias_grad,
        router_grad,
        in_grad,
        back_grad,
    ) = totals
    offset_grad = bias_pull(bias_grad)[0]
    rel_grad = jnp.dot(picks.T, offset_grad.T, precision=HIGHEST)
    gains = jnp.stack([attn_grad, ffn_grad], axis=1)
    shares = (
        lax.psum_scatter(
            query_wgrad.astype(jnp.bfloat16), "expert", scatter_dimension=0, tiled=True
        ).astype(jnp.float32),
        lax.psum_scatter(
            key_wgrad.astype(jnp.bfloat16), "expert", scatter_dimension=0, tiled=True
        ).astype(jnp.float32),
        lax.psum_scatter(
            value_wgrad.astype(jnp.bfloat16), "expert", scatter_dimension=0, tiled=True
        ).astype(jnp.float32),
        lax.psum_scatter(
            out_grad.T.astype(jnp.bfloat16), "expert", scatter_dimension=0, tiled=True
        ).astype(jnp.float32),
        lax.psum_scatter(
            gains.astype(jnp.bfloat16), "expert", scatter_dimension=0, tiled=True
        ).astype(jnp.float32),
        lax.psum_scatter(
            router_grad.astype(jnp.bfloat16), "expert", scatter_dimension=0, tiled=True
        ).astype(jnp.float32),
        lax.psum_scatter(
            rel_grad.astype(jnp.bfloat16), "expert", scatter_dimension=0, tiled=True
        ).astype(jnp.float32),
    )
    return (
        acts[None],
        input_grads[None],
        shares[4][:, 0][None],
        shares[4][:, 1][None],
        shares[0][None],
        shares[1][None],
        shares[2][None],
        shares[3].T[None],
        shares[6][None],
        shares[5][None],
        in_grad[None],
        back_grad[None],
    )


def solution(mesh):
    placed = (
        P(None, "expert", None),
        P(None, "expert", None),
        P("section", None),
        P("section", None),
        P("section", None, "tensor"),
        P("section", None, "tensor"),
        P("section", None, "tensor"),
        P("section", "tensor", None),
        P("section", None, "tensor"),
        P("section", None, None),
        P("section", "expert", None, "tensor"),
        P("section", "expert", "tensor", None),
        P("section", None, "expert", None),
        P("section", None, "expert"),
    )
    return jax.shard_map(
        body,
        mesh=mesh,
        in_specs=placed,
        out_specs=(
            P("section", None, "expert", None),
            P("section", None, "expert", None),
            P("section", "expert"),
            P("section", "expert"),
            P("section", "expert", "tensor"),
            P("section", "expert", "tensor"),
            P("section", "expert", "tensor"),
            P("section", "tensor", "expert"),
            P("section", "expert", "tensor"),
            P("section", "expert", None),
            P("section", "expert", None, "tensor"),
            P("section", "expert", "tensor", None),
        ),
        check_vma=False,
    )
```

profile of v0, /device:TPU:0, one launch (start us, length us, event | category | flops | bytes accessed | tf_op | source)
XLA Modules:
  0.0 4574.4 jit_solution(1450817507444755202)
XLA Ops:
  24.3 860.2 %gather_fusion = f32[262144,3]{1,0:T(8,128)} fusion(f32[3,1023]{0,1:T(8,128)S(1)} %copy.279, s32[262144]{0:T(1024)S(1)} %broadcast_clamp_fusion), kind=kCustom, calls=%fused_computation | custom fusion | bytes 7340032 | tf_op jit(solution)/shard_map/jvp()/gather | solution.py:326
  884.5 70.3 %copy.280 = f32[512,512,3]{0,1,2:T(8,128)S(1)} copy(f32[512,512,3]{2,1,0:T(8,128)} %bitcast.7) | data formatting | bytes 6291456 | tf_op jit(solution)/shard_map/jvp()/gather | solution.py:326
  975.5 51.9 %all-reduce.14.cloned.1.call-done = bf16[1024,768]{1,0:T(8,128)(2,1)} async-done(((bf16[1024,768]{1,0:T(8,128)(2,1)}), bf16[1024,768]{1,0:T(8,128)(2,1)}) %all-reduce.14.cloned.1.call-update) | async-done | bytes 1572880 | tf_op jit(solution)/shard_map/psum | solution.py:89
  1035.8 58.7 %all_to_all.60 = bf16[4,4,96,768]{3,2,0,1:T(8,128)(2,1)S(1)} all-to-all(bf16[4,4,96,768]{3,2,0,1:T(8,128)(2,1)S(1)} %copy.286), channel_id=1, replica_groups=mesh['section'=2,'expert'=4,'tensor'=4] {'expert'}, dimensions={1} | all-to-all | bytes 4718592 | tf_op jit(solution)/shard_map/all_to_all | solution.py:117
  1113.3 159.4 %all-reduce.29 = bf16[4,384,768]{2,1,0:T(8,128)(2,1)} all-reduce(f32[4,384,768]{2,1,0:T(8,128)} %fusion.37), channel_id=1, replica_groups=mesh['section'=2,'expert'=4,'tensor'=4] {'tensor'}, use_global_device_ids=true, to_apply=%region_11.12 | all-reduce | flops 1179648 | bytes 7077888 | tf_op jit(solution)/shard_map/psum | solution.py:123
  1283.7 48.4 %all-to-all-done.1 = bf16[4,4,96,768]{3,2,0,1:T(8,128)(2,1)} async-done(((bf16[4,4,96,768]{3,2,0,1:T(8,128)(2,1)}), bf16[4,4,96,768]{3,2,0,1:T(8,128)(2,1)}, u32[]{:S(2)}, u32[]{:S(2)}) %all-to-all-start.1) | async-done | bytes 2359328 | tf_op jit(solution)/shard_map/all_to_all | solution.py:124
  1382.0 41.9 all-reduce.16.cloned.1.call-done
  1432.8 58.6 %all_to_all.61 = bf16[4,4,96,768]{3,2,0,1:T(8,128)(2,1)S(1)} all-to-all(bf16[4,4,96,768]{3,2,0,1:T(8,128)(2,1)S(1)} %copy.298), channel_id=1, replica_groups=mesh['section'=2,'expert'=4,'tensor'=4] {'expert'}, dimensions={1} | all-to-all | bytes 4718592 | tf_op jit(solution)/shard_map/all_to_all | solution.py:117
  1514.7 159.4 %all-reduce.30 = bf16[4,384,768]{2,1,0:T(8,128)(2,1)} all-reduce(f32[4,384,768]{2,1,0:T(8,128)} %fusion.35), channel_id=1, replica_groups=mesh['section'=2,'expert'=4,'tensor'=4] {'tensor'}, use_global_device_ids=true, to_apply=%region_23.24 | all-reduce | flops 1179648 | bytes 7077888 | tf_op jit(solution)/shard_map/psum | solution.py:123
  1685.2 48.6 %all-to-all-done.3 = bf16[4,4,96,768]{3,2,0,1:T(8,128)(2,1)} async-done(((bf16[4,4,96,768]{3,2,0,1:T(8,128)(2,1)}), bf16[4,4,96,768]{3,2,0,1:T(8,128)(2,1)}, u32[]{:S(2)}, u32[]{:S(2)}) %all-to-all-start.3) | async-done | bytes 2359328 | tf_op jit(solution)/shard_map/all_to_all | solution.py:124
  1765.6 40.4 all-to-all-done.6
  1820.9 72.3 %all-reduce.18.cloned.1.call-done = bf16[4,4,96,768]{3,2,0,1:T(8,128)(2,1)} async-done(((bf16[4,4,96,768]{3,2,0,1:T(8,128)(2,1)}), bf16[4,4,96,768]{3,2,0,1:T(8,128)(2,1)}) %all-reduce.18.cloned.1.call-update) | async-done | bytes 2359312 | tf_op jit(solution)/shard_map/psum | solution.py:207
  1908.9 43.0 all-to-all-done.7
  2038.5 71.9 %all-reduce.28.cloned.1.call-done = (bf16[1024,768]{1,0:T(8,128)(2,1)}, bf16[1024,768]{1,0:T(8,128)(2,1)}) async-done(((bf16[1024,768]{1,0:T(8,128)(2,1)}, bf16[1024,768]{1,0:T(8,128)(2,1)}), (bf16[1024,768]{1,0:T(8,128)(2,1)}, bf16[1024,768]{1,0:T(8,128)(2,1)})) %all-reduce.28.cloned.1.call-update) | async-done | bytes 3145744 | tf_op jit(solution)/shard_map/psum | solution.py:89
  2119.4 58.2 %all_to_all.62 = bf16[4,4,96,768]{3,2,0,1:T(8,128)(2,1)S(1)} all-to-all(bf16[4,4,96,768]{3,2,0,1:T(8,128)(2,1)S(1)} %copy.310), channel_id=1, replica_groups=mesh['section'=2,'expert'=4,'tensor'=4] {'expert'}, dimensions={1} | all-to-all | bytes 4718592 | tf_op jit(solution)/shard_map/all_to_all | solution.py:117
  2208.0 157.9 %all-reduce.31 = bf16[4,384,768]{2,1,0:T(8,128)(2,1)} all-reduce(f32[4,384,768]{2,1,0:T(8,128)} %fusion.33), channel_id=1, replica_groups=mesh['section'=2,'expert'=4,'tensor'=4] {'tensor'}, use_global_device_ids=true, to_apply=%region_35.36 | all-reduce | flops 1179648 | bytes 7077888 | tf_op jit(solution)/shard_map/psum | solution.py:123
  2388.1 35.0 all-to-all-done.5
  2456.5 38.6 all-to-all-done.8
  2512.5 73.9 %all-reduce.20.cloned.1.call-done = bf16[4,4,96,768]{3,2,0,1:T(8,128)(2,1)} async-done(((bf16[4,4,96,768]{3,2,0,1:T(8,128)(2,1)}), bf16[4,4,96,768]{3,2,0,1:T(8,128)(2,1)}) %all-reduce.20.cloned.1.call-update) | async-done | bytes 2359312 | tf_op jit(solution)/shard_map/psum | solution.py:207
  2603.4 41.7 all-to-all-done.9
  2689.2 51.4 %all-reduce.22.cloned.1.call-done = bf16[1024,768]{1,0:T(8,128)(2,1)} async-done(((bf16[1024,768]{1,0:T(8,128)(2,1)}), bf16[1024,768]{1,0:T(8,128)(2,1)}) %all-reduce.22.cloned.1.call-update) | async-done | bytes 1572880 | tf_op jit(solution)/shard_map/psum | solution.py:273
  2906.6 45.5 all-reduce.24.cloned.1.call-done
  3076.7 61.2 %copy.406 = f32[512,512,3]{2,1,0:T(8,128)} copy(f32[512,512,3]{0,1,2:T(8,128)} %add_bitcast_fusion.2) | data formatting | bytes 6291456 | tf_op jit(solution)/shard_map/add | solution.py:370
  3137.9 1387.2 %scatter_custom_fusion = f32[3,1023]{0,1:T(8,128)} fusion(s32[262144]{0:T(1024)} %constant.259, f32[262144,3]{1,0:T(8,128)} %bitcast.90, f32[]{:T(128)} %constant.199.clone.1), kind=kCustom, calls=%fused_computation.650 | custom fusion | flops 786432 | bytes 12788 | tf_op jit(solution)/shard_map/transpose(jvp())/scatter-add | solution.py:326
  (943 shorter events, 820.0 us)
Async XLA Ops:
  7.2 1020.2 %all-reduce.14.cloned.1.call-start = ((), (), s32[]{:S(2)}) async-start(), calls=%async_computation.18 | async-start | bytes 3145728 | tf_op jit(solution)/shard_map/psum | solution.py:89
  1275.9 56.3 %all-to-all-start.1 = ((bf16[4,4,96,768]{3,2,0,1:T(8,128)(2,1)}), bf16[4,4,96,768]{3,2,0,1:T(8,128)(2,1)}, u32[]{:S(2)}, u32[]{:S(2)}) async-start(bf16[4,4,96,768]{3,2,0,1:T(8,128)(2,1)} %copy.288), calls=%async_computation.1 | async-start | bytes 4718592 | tf_op jit(solution)/shard_map/all_to_all | solution.py:124
  1280.3 143.6 %all-reduce.16.cloned.1.call-start = ((), (), s32[]{:S(2)}) async-start(), calls=%async_computation.19 | async-start | bytes 3145728 | tf_op jit(solution)/shard_map/psum | solution.py:89
  1677.3 56.5 %all-to-all-start.3 = ((bf16[4,4,96,768]{3,2,0,1:T(8,128)(2,1)}), bf16[4,4,96,768]{3,2,0,1:T(8,128)(2,1)}, u32[]{:S(2)}, u32[]{:S(2)}) async-start(bf16[4,4,96,768]{3,2,0,1:T(8,128)(2,1)} %copy.300), calls=%async_computation.3 | async-start | bytes 4718592 | tf_op jit(solution)/shard_map/all_to_all | solution.py:124
  1748.8 57.2 %all-to-all-start.6 = ((bf16[4,4,96,768]{3,2,0,1:T(8,128)(2,1)}), bf16[4,4,96,768]{3,2,0,1:T(8,128)(2,1)}, u32[]{:S(2)}, u32[]{:S(2)}) async-start(bf16[4,4,96,768]{3,2,0,1:T(8,128)(2,1)} %copy.315), calls=%async_computation.6 | async-start | bytes 4718592 | tf_op jit(solution)/shard_map/all_to_all | solution.py:197
  1753.2 140.0 %all-reduce.18.cloned.1.call-start = ((), (), s32[]{:S(2)}) async-start(), calls=%async_computation.20 | async-start | bytes 4718592 | tf_op jit(solution)/shard_map/psum | solution.py:207
  1893.3 58.7 %all-to-all-start.7 = ((bf16[4,4,96,768]{3,2,0,1:T(8,128)(2,1)}), bf16[4,4,96,768]{3,2,0,1:T(8,128)(2,1)}, u32[]{:S(2)}, u32[]{:S(2)}) async-start(bf16[4,4,96,768]{3,2,0,1:T(8,128)(2,1)} %all-reduce.18.cloned.1.call-done), calls=%async_computation.7 | async-start | bytes 4718592 | tf_op jit(solution)/shard_map/all_to_all | solution.py:208
  1897.9 212.5 %all-reduce.28.cloned.1.call-start = ((), (), s32[]{:S(2)}) async-start(), calls=%async_computation.31 | async-start | bytes 6291456 | tf_op jit(solution)/shard_map/psum | solution.py:89
  1904.8 53.7 %collective-permute-start.1 = (bf16[1024,768]{1,0:T(8,128)(2,1)}, bf16[1024,768]{1,0:T(8,128)(2,1)}, u32[]{:S(2)}, u32[]{:S(2)}) collective-permute-start(bf16[1024,768]{1,0:T(8,128)(2,1)} %get-tuple-element.128), channel_id=1, source_target_pairs={{0,16},{1,17},{2,18},{3,19},{4,20},{5,21},{6,22},{7,23},{8,24},{9,... | collective-permute-start | bytes 4718600 | tf_op jit(solution)/shard_map/ppermute | solution.py:18
  2369.1 53.9 %all-to-all-start.5 = ((bf16[4,4,96,768]{3,2,0,1:T(8,128)(2,1)}), bf16[4,4,96,768]{3,2,0,1:T(8,128)(2,1)}, u32[]{:S(2)}, u32[]{:S(2)}) async-start(bf16[4,4,96,768]{3,2,0,1:T(8,128)(2,1)} %copy.312), calls=%async_computation.5 | async-start | bytes 4718592 | tf_op jit(solution)/shard_map/all_to_all | solution.py:124
  2439.5 55.6 %all-to-all-start.8 = ((bf16[4,4,96,768]{3,2,0,1:T(8,128)(2,1)}), bf16[4,4,96,768]{3,2,0,1:T(8,128)(2,1)}, u32[]{:S(2)}, u32[]{:S(2)}) async-start(bf16[4,4,96,768]{3,2,0,1:T(8,128)(2,1)} %copy.334), calls=%async_computation.8 | async-start | bytes 4718592 | tf_op jit(solution)/shard_map/all_to_all | solution.py:197
  2444.0 142.4 %all-reduce.20.cloned.1.call-start = ((), (), s32[]{:S(2)}) async-start(), calls=%async_computation.21 | async-start | bytes 4718592 | tf_op jit(solution)/shard_map/psum | solution.py:207
  2586.4 58.7 %all-to-all-start.9 = ((bf16[4,4,96,768]{3,2,0,1:T(8,128)(2,1)}), bf16[4,4,96,768]{3,2,0,1:T(8,128)(2,1)}, u32[]{:S(2)}, u32[]{:S(2)}) async-start(bf16[4,4,96,768]{3,2,0,1:T(8,128)(2,1)} %all-reduce.20.cloned.1.call-done), calls=%async_computation.9 | async-start | bytes 4718592 | tf_op jit(solution)/shard_map/all_to_all | solution.py:208
  2591.0 149.6 %all-reduce.22.cloned.1.call-start = ((), (), s32[]{:S(2)}) async-start(), calls=%async_computation.22 | async-start | bytes 3145728 | tf_op jit(solution)/shard_map/psum | solution.py:273
  2793.6 61.0 %all-to-all-start.10 = ((bf16[4,4,96,768]{3,2,0,1:T(8,128)(2,1)}), bf16[4,4,96,768]{3,2,0,1:T(8,128)(2,1)}, u32[]{:S(2)}, u32[]{:S(2)}) async-start(bf16[4,4,96,768]{3,2,0,1:T(8,128)(2,1)} %copy.353), calls=%async_computation.10 | async-start | bytes 4718592 | tf_op jit(solution)/shard_map/all_to_all | solution.py:197
  2798.3 92.4 %reduce-scatter.22.cloned.1.call-start = ((), (), s32[]{:S(2)}) async-start(), calls=%async_computation.30 | async-start | bytes 245760
  2825.0 127.1 %all-reduce.24.cloned.1.call-start = ((), (), s32[]{:S(2)}) async-start(), calls=%async_computation.23 | async-start | bytes 4718592 | tf_op jit(solution)/shard_map/psum | solution.py:207
  2952.0 58.7 %all-to-all-start.11 = ((bf16[4,4,96,768]{3,2,0,1:T(8,128)(2,1)}), bf16[4,4,96,768]{3,2,0,1:T(8,128)(2,1)}, u32[]{:S(2)}, u32[]{:S(2)}) async-start(bf16[4,4,96,768]{3,2,0,1:T(8,128)(2,1)} %all-reduce.24.cloned.1.call-done), calls=%async_computation.11 | async-start | bytes 4718592 | tf_op jit(solution)/shard_map/all_to_all | solution.py:208
  2956.6 1580.7 %reduce-scatter.18.cloned.1.call-start = ((), (), s32[]{:S(2)}) async-start(), calls=%async_computation.28 | async-start | bytes 491520 | tf_op jit(solution)/shard_map/reduce_scatter | solution.py:398
  3044.4 1496.3 %reduce-scatter.16.cloned.1.call-start = ((), (), s32[]{:S(2)}) async-start(), calls=%async_computation.27 | async-start | bytes 491520 | tf_op jit(solution)/shard_map/reduce_scatter | solution.py:395
  3057.0 1485.3 %reduce-scatter.14.cloned.1.call-start = ((), (), s32[]{:S(2)}) async-start(), calls=%async_computation.26 | async-start | bytes 491520 | tf_op jit(solution)/shard_map/reduce_scatter | solution.py:392
  3061.5 1482.3 %reduce-scatter.12.cloned.1.call-start = ((), (), s32[]{:S(2)}) async-start(), calls=%async_computation.25 | async-start | bytes 491520 | tf_op jit(solution)/shard_map/reduce_scatter | solution.py:389
  3065.9 1479.6 %all-reduce.26.cloned.1.call-start = ((), (), s32[]{:S(2)}) async-start(), calls=%async_computation.24 | async-start | bytes 3145728 | tf_op jit(solution)/shard_map/psum | solution.py:273
  3071.0 1495.0 %reduce-scatter.20.cloned.1.call-start = ((), (), s32[]{:S(2)}) async-start(), calls=%async_computation.29 | async-start | bytes 245760
  (296 other events, 21680.7 us)
Sparse Core Ops, SparseCore 0:
  963.8 63.5 all-reduce.13
  1364.7 59.1 all-reduce.15
  1821.1 72.1 all-reduce.17
  2024.7 85.5 all-reduce.27
  2512.6 73.7 all-reduce.19
  2681.5 59.0 all-reduce.21
  2825.1 30.7 reduce-scatter.21
  2879.8 72.1 all-reduce.23
  3044.5 18.7 reduce-scatter.17
  3065.5 18.8 reduce-scatter.15
  3086.7 18.8 reduce-scatter.13
  3107.8 18.8 reduce-scatter.11
  3129.8 59.1 all-reduce.25
  4549.3 16.5 reduce-scatter.19
where the time goes:
time: 4580 us; the launch traced here: 4570 us
  other arithmetic  1550 us (34%)
  local copies, waits for them, and re-layouts  1140 us (25%)
  waiting for transfers between devices  783 us (17%)
  blocking collectives  662 us (14%)
  matrix products  368 us (8%)
  starting transfers between devices  50.2 us (1%)
    scatter-add x1, other arithmetic, make_bias(): return table_rows[:, index_grid]  1390 us
    gather x2, local copies, waits for them, and re-layouts, make_bias(): return table_rows[:, index_grid]  930 us
    psum x3, blocking collectives, layer_forward(): expert_out = lax.psum(partial_out, 'tensor').astype(jnp.bfloat16)  477 us
    psum x3, waiting for transfers between devices, layer_backward(): input_low = lax.psum(input_part.astype(jnp.bfloat16), 'tensor')  192 us
    all_to_all x3, blocking collectives, layer_forward(): lax.all_to_all(outgoing, 'expert', split_axis=1, concat_axis=1, tiled=True)  176 us
    psum x3, waiting for transfers between devices, layer_forward(): lax.psum(jnp.dot(mixed_low, w_out, preferred_element_type=jnp.float32).as...  166 us
    all_to_all x3, waiting for transfers between devices, layer_forward(): lax.all_to_all(expert_out.reshape(local, groups, capacity, width), 'exper...  132 us
    all_to_all x3, waiting for transfers between devices, layer_backward(): lax.all_to_all(input_low.reshape(local, groups, capacity, width), 'expert...  119 us
  transfers between devices with their start and end apart: 27, of which 18 were waited for; matrix products, arithmetic and copies ran while one was open for 38% of the time, Pallas kernels for 0%

commit v1 on v0

v1 whole, which is shorter than its diff:
```python
import functools
import jax
import jax.numpy as jnp
import numpy as np
from jax import lax
from jax.experimental import pallas as pl
from jax.experimental.pallas import tpu as pltpu
from jax.sharding import PartitionSpec as P

DH = 64
LENGTH = 512
TILE = 128
EPSILON = 1e-06
BF16 = jnp.bfloat16
F32 = jnp.float32


def bucket_starts():
    starts = list(range(1, 9))
    for ladder in range(1, 8):
        distance = 8
        while distance**8 < 2 ** (24 + 4 * ladder):
            distance = distance + 1
        starts.append(distance)
    return starts


STARTS = bucket_starts()
HALF = len(STARTS) + 1


def root_mean(values):
    return lax.rsqrt(jnp.mean(values * values, axis=-1, keepdims=True) + EPSILON)


def dot(left, right):
    return jnp.dot(left, right, preferred_element_type=F32)


def dot_left(left, right):
    return lax.dot_general(left, right, (((0,), (0,)), ((), ())), preferred_element_type=F32)


def dot_right(left, right):
    return lax.dot_general(left, right, (((1,), (1,)), ((), ())), preferred_element_type=F32)


def offset_block(delta):
    rows = lax.broadcasted_iota(jnp.int32, (TILE, TILE), 0)
    cols = lax.broadcasted_iota(jnp.int32, (TILE, TILE), 1)
    return rows - cols + delta * TILE


def fill_bias(rel_ref, bias_ref, heads):
    tiles = LENGTH // TILE
    for delta in (-1, 0, 1):
        offset = offset_block(delta)
        blocks = [jnp.full((TILE, TILE), rel_ref[0, h], F32) for h in range(heads)]
        for step, start in enumerate(STARTS):
            if delta <= 0:
                mask = offset <= -start
                blocks = [
                    jnp.where(mask, rel_ref[step + 1, h], block) for h, block in enumerate(blocks)
                ]
            if delta >= 0:
                mask = offset >= start
                blocks = [
                    jnp.where(mask, rel_ref[HALF + step + 1, h], block)
                    for h, block in enumerate(blocks)
                ]
        for h in range(heads):
            for i in range(tiles):
                j = i - delta
                if 0 <= j < tiles:
                    bias_ref[h, i * TILE : (i + 1) * TILE, j * TILE : (j + 1) * TILE] = blocks[h]
    for h in range(heads):
        above = jnp.full((TILE, TILE), rel_ref[2 * HALF - 1, h], F32)
        below = jnp.full((TILE, TILE), rel_ref[HALF - 1, h], F32)
        for i in range(tiles):
            for j in range(tiles):
                if abs(i - j) > 1:
                    bias_ref[h, i * TILE : (i + 1) * TILE, j * TILE : (j + 1) * TILE] = (
                        above if i > j else below
                    )


def attend_kernel(rel_ref, qkv_ref, mixed_ref, lse_ref, bias_ref, *, heads):
    @pl.when(pl.program_id(0) == 0)
    def _():
        fill_bias(rel_ref, bias_ref, heads)

    cols = heads * DH
    outs = []
    for h in range(heads):
        query = qkv_ref[:, h * DH : (h + 1) * DH]
        keys = qkv_ref[:, cols + h * DH : cols + (h + 1) * DH]
        values = qkv_ref[:, 2 * cols + h * DH : 2 * cols + (h + 1) * DH]
        scores = dot_right(keys, query) * 0.125 + bias_ref[h]
        highest = jnp.max(scores, axis=0, keepdims=True)
        raised = jnp.exp(scores - highest)
        total = jnp.sum(raised, axis=0, keepdims=True)
        probs = (raised * (1.0 / total)).astype(BF16)
        outs.append(dot_left(probs, values).astype(BF16))
        lse_ref[0, h : h + 1, :] = highest + jnp.log(total)
    mixed_ref[...] = jnp.concatenate(outs, axis=1)


def attend(qkv, rel):
    rows = qkv.shape[0]
    heads = rel.shape[1]
    cols = heads * DH
    sequences = rows // LENGTH
    return pl.pallas_call(
        functools.partial(attend_kernel, heads=heads),
        grid=(sequences,),
        in_specs=[
            pl.BlockSpec(memory_space=pltpu.SMEM),
            pl.BlockSpec((LENGTH, 3 * cols), lambda s: (s, 0)),
        ],
        out_specs=[
            pl.BlockSpec((LENGTH, cols), lambda s: (s, 0)),
            pl.BlockSpec((1, heads, LENGTH), lambda s: (s, 0, 0)),
        ],
        out_shape=[
            jax.ShapeDtypeStruct((rows, cols), BF16),
            jax.ShapeDtypeStruct((sequences, heads, LENGTH), F32),
        ],
        scratch_shapes=[pltpu.VMEM((heads, LENGTH, LENGTH), F32)],
        compiler_params=pltpu.CompilerParams(
            dimension_semantics=("arbitrary",), vmem_limit_bytes=40 << 20
        ),
    )(rel, qkv)


def attend_back_kernel(
    rel_ref, qkv_ref, lse_ref, grad_ref, dqkv_ref, drel_ref, bias_ref, near_ref, *, heads
):
    tiles = LENGTH // TILE

    @pl.when(pl.program_id(0) == 0)
    def _():
        fill_bias(rel_ref, bias_ref, heads)
        near_ref[...] = jnp.zeros_like(near_ref)

    cols = heads * DH
    dqs, dks, dvs = [], [], []
    for h in range(heads):
        query = qkv_ref[:, h * DH : (h + 1) * DH]
        keys = qkv_ref[:, cols + h * DH : cols + (h + 1) * DH]
        values = qkv_ref[:, 2 * cols + h * DH : 2 * cols + (h + 1) * DH]
        grad = grad_ref[:, h * DH : (h + 1) * DH]
        scores = dot_right(keys, query) * 0.125 + bias_ref[h]
        probs = jnp.exp(scores - lse_ref[0, h : h + 1, :])
        dvs.append(dot(probs.astype(BF16), grad).astype(BF16))
        dprobs = dot_right(values, grad)
        weighted = jnp.sum(probs * dprobs, axis=0, keepdims=True)
        dscores = (probs * (dprobs - weighted)).astype(BF16)
        dks.append((dot(dscores, query) * 0.125).astype(BF16))
        dqs.append((dot_left(dscores, keys) * 0.125).astype(BF16))
        wide = dscores.astype(F32)
        sums = [None] * 5
        for i in range(tiles):
            for j in range(tiles):
                place = max(-2, min(2, i - j)) + 2
                block = wide[i * TILE : (i + 1) * TILE, j * TILE : (j + 1) * TILE]
                sums[place] = block if sums[place] is None else sums[place] + block
        for place in range(5):
            near_ref[h, place] = near_ref[h, place] + sums[place]
    dqkv_ref[...] = jnp.concatenate(dqs + dks + dvs, axis=1)

    @pl.when(pl.program_id(0) == pl.num_programs(0) - 1)
    def _():
        edges = STARTS + [1 << 20]
        for h in range(heads):
            rows = [jnp.zeros((1, TILE), F32) for _ in range(2 * HALF)]
            for delta in (-1, 0, 1):
                offset = offset_block(delta)
                block = near_ref[h, delta + 2]
                if delta == 0:
                    rows[0] = jnp.sum(
                        jnp.where(offset == 0, block, 0.0), axis=0, keepdims=True
                    )
                for step in range(HALF - 1):
                    if delta <= 0:
                        mask = (offset <= -edges[step]) & (offset > -edges[step + 1])
                        rows[step + 1] = rows[step + 1] + jnp.sum(
                            jnp.where(mask, block, 0.0), axis=0, keepdims=True
                        )
                    if delta >= 0:
                        mask = (offset >= edges[step]) & (offset < edges[step + 1])
                        rows[HALF + step + 1] = rows[HALF + step + 1] + jnp.sum(
                            jnp.where(mask, block, 0.0), axis=0, keepdims=True
                        )
            rows[HALF - 1] = rows[HALF - 1] + jnp.sum(near_ref[h, 0], axis=0, keepdims=True)
            rows[2 * HALF - 1] = rows[2 * HALF - 1] + jnp.sum(
                near_ref[h, 4], axis=0, keepdims=True
            )
            drel_ref[h] = jnp.concatenate(rows, axis=0)


def attend_back(qkv, rel, lse, grad):
    rows = qkv.shape[0]
    heads = rel.shape[1]
    cols = heads * DH
    sequences = rows // LENGTH
    return pl.pallas_call(
        functools.partial(attend_back_kernel, heads=heads),
        grid=(sequences,),
        in_specs=[
            pl.BlockSpec(memory_space=pltpu.SMEM),
            pl.BlockSpec((LENGTH, 3 * cols), lambda s: (s, 0)),
            pl.BlockSpec((1, heads, LENGTH), lambda s: (s, 0, 0)),
            pl.BlockSpec((LENGTH, cols), lambda s: (s, 0)),
        ],
        out_specs=[
            pl.BlockSpec((LENGTH, 3 * cols), lambda s: (s, 0)),
            pl.BlockSpec((heads, 2 * HALF, TILE), lambda s: (0, 0, 0)),
        ],
        out_shape=[
            jax.ShapeDtypeStruct((rows, 3 * cols), BF16),
            jax.ShapeDtypeStruct((heads, 2 * HALF, TILE), F32),
        ],
        scratch_shapes=[
            pltpu.VMEM((heads, LENGTH, LENGTH), F32),
            pltpu.VMEM((heads, 5, TILE, TILE), F32),
        ],
        compiler_params=pltpu.CompilerParams(
            dimension_semantics=("arbitrary",), vmem_limit_bytes=40 << 20
        ),
    )(rel, qkv, lse, grad)


def swap_tensor(block, distance):
    devices = lax.axis_size("tensor")
    return lax.ppermute(block, "tensor", [(i, i ^ distance) for i in range(devices)])


def gather_tensor(block):
    return [block] + [swap_tensor(block, d) for d in range(1, lax.axis_size("tensor"))]


def exchange_tensor(blocks):
    return [blocks[0]] + [swap_tensor(blocks[d], d) for d in range(1, len(blocks))]


def swap_section(block):
    return lax.ppermute(block, "section", [(0, 1), (1, 0)])


def swap_experts(block):
    return lax.all_to_all(block, "expert", split_axis=0, concat_axis=0, tiled=True)


def sum_blocks(blocks):
    total = blocks[0].astype(F32)
    for block in blocks[1:]:
        total = total + block.astype(F32)
    return total


def make_plan(route_rows, keep_rows, experts, capacity):
    tokens = route_rows.shape[0]
    devices = lax.axis_size("tensor")
    rank = lax.axis_index("tensor")
    owned = tokens // devices
    share = capacity // devices
    ids = jnp.arange(experts, dtype=jnp.int32)
    chosen = route_rows[:, None] == ids[None, :]
    order = jnp.arange(tokens, dtype=jnp.int32)
    lower = (order[:, None] > order[None, :]).astype(BF16)
    before = dot(lower, chosen.astype(BF16))
    chosen_f = chosen.astype(F32)
    counts = jnp.sum(chosen_f, axis=0)
    starts = jnp.sum(jnp.where(ids[None, :] < ids[:, None], counts[None, :], 0.0), axis=1)
    position = jnp.sum(chosen_f * (before + starts[None, :]), axis=1).astype(jnp.int32)
    distances = jnp.arange(devices, dtype=jnp.int32)
    rows = jnp.arange(owned, dtype=jnp.int32)
    wanted = (rows[None, :] * devices + (rank ^ distances)[:, None]).reshape(-1)
    deal = (wanted[:, None] == position[None, :]).astype(BF16)
    mine = wanted[:owned, None] == position[None, :]
    route_own = jnp.sum(jnp.where(mine, route_rows[None, :], 0), axis=1, dtype=jnp.int32)
    keep_own = jnp.sum(jnp.where(mine, keep_rows[None, :], 0), axis=1, dtype=jnp.int32)
    chosen_own = route_own[:, None] == ids[None, :]
    first = (starts.astype(jnp.int32) - rank + devices - 1) // devices
    slot = rows - jnp.sum(jnp.where(chosen_own, first[None, :], 0), axis=1, dtype=jnp.int32)
    slot = jnp.where(keep_own > 0, route_own * share + slot, -1)
    place = (jnp.arange(experts * share, dtype=jnp.int32)[:, None] == slot[None, :]).astype(BF16)
    return (deal, deal[:owned], place, chosen_own.astype(F32), keep_own.astype(F32))


def to_experts(rows, place, local):
    groups = lax.axis_size("expert")
    width = rows.shape[1]
    sent = dot(place, rows).astype(BF16).reshape(groups, -1, width)
    got = swap_experts(sent)
    share = got.shape[1] // local
    got = got.reshape(groups, local, share, width).transpose(1, 0, 2, 3)
    got = got.reshape(local, groups * share, width)
    return jnp.concatenate(gather_tensor(got), axis=1)


def from_experts(parts, place):
    groups = lax.axis_size("expert")
    devices = lax.axis_size("tensor")
    local, slots, width = parts.shape
    own = slots // devices
    parts = parts.astype(BF16)
    blocks = exchange_tensor([parts[:, d * own : (d + 1) * own] for d in range(devices)])
    summed = sum_blocks(blocks).astype(BF16)
    summed = summed.reshape(local, groups, own // groups, width).transpose(1, 0, 2, 3)
    back = swap_experts(summed.reshape(groups, -1, width)).reshape(-1, width)
    return dot_left(place, back)


def per_expert(left, right, contract):
    return lax.dot_general(
        left, right, ((contract[:1], contract[1:]), ((0,), (0,))), preferred_element_type=F32
    )


def layer_forward(rows_in, weights, rel, plan):
    attn_gain, ffn_gain, w_qkv, w_out, w_router, w_in, w_back = weights
    deal, deal_own, place, chosen, kept = plan
    devices = lax.axis_size("tensor")
    local = w_in.shape[0]
    layer_in = rows_in.astype(F32)
    scale_one = root_mean(layer_in)
    normed = (layer_in * scale_one * attn_gain).astype(BF16)
    qkv = dot(normed, w_qkv).astype(BF16)
    mixed, lse = attend(qkv, rel)
    cols = mixed.shape[1]
    dealt = dot(deal, mixed).astype(BF16).reshape(devices, -1, cols)
    heads = exchange_tensor([dealt[d] for d in range(devices)])
    own_in = dot(deal_own, rows_in)
    branch = sum(dot(heads[d], w_out[d]) for d in range(devices))
    middle = own_in + branch
    scale_two = root_mean(middle)
    normed_two = (middle * scale_two * ffn_gain).astype(BF16)
    probs = jax.nn.softmax(dot(normed_two, w_router), axis=-1)
    gate = jnp.sum(probs * chosen, axis=-1)
    incoming = to_experts(normed_two, place, local)
    inner = per_expert(incoming, w_in, (2, 1))
    cumulative = 0.5 * (1.0 + lax.erf(inner * np.float32(np.sqrt(0.5))))
    density = jnp.exp(-0.5 * inner * inner) * np.float32(1.0 / np.sqrt(2.0 * np.pi))
    hidden = (inner * cumulative).astype(BF16)
    slope = (cumulative + inner * density).astype(BF16)
    per_token = from_experts(per_expert(hidden, w_back, (2, 1)), place)
    output = (middle + (kept * gate)[:, None] * per_token).astype(BF16)
    every = jnp.concatenate(gather_tensor(output), axis=0)
    rows_out = dot_left(deal, every).astype(BF16)
    saved = (own_in, normed, qkv, lse, heads, middle, normed_two, probs, gate)
    return (rows_out, saved + (incoming, hidden, slope, per_token))


def norm_back(grad, values, gain):
    scale = root_mean(values)
    scaled = grad * gain
    values_grad = scale * scaled - values * (scale * scale * scale) * jnp.mean(
        scaled * values, axis=-1, keepdims=True
    )
    return (values_grad, jnp.sum(grad * values * scale, axis=0))


def layer_backward(saved, rows_grad, weights, rel, plan):
    attn_gain, ffn_gain, w_qkv, w_out, w_router, w_in, w_back = weights
    deal, deal_own, place, chosen, kept = plan
    own_in, normed, qkv, lse, heads, middle, normed_two, probs, gate = saved[:9]
    incoming, hidden, slope, per_token = saved[9:]
    devices = lax.axis_size("tensor")
    local = w_in.shape[0]
    grad_out = dot(deal_own, rows_grad)
    gated = ((kept * gate)[:, None] * grad_out).astype(BF16)
    gate_grad = kept * jnp.sum(grad_out * per_token, axis=-1)
    expert_grad = to_experts(gated, place, local)
    hidden_grad = per_expert(expert_grad, w_back, (2, 2))
    inner_grad = (hidden_grad * slope.astype(F32)).astype(BF16)
    input_rows = from_experts(per_expert(inner_grad, w_in, (2, 2)), place)
    back_grad = per_expert(hidden, expert_grad, (1, 1))
    in_grad = per_expert(incoming, inner_grad, (1, 1))
    logit_grad = (probs * (chosen - gate[:, None]) * gate_grad[:, None]).astype(BF16)
    router_grad = dot_left(normed_two, logit_grad)
    normed_two_grad = input_rows + dot_right(logit_grad, w_router)
    middle_part, ffn_grad = norm_back(normed_two_grad, middle, ffn_gain)
    middle_grad = grad_out + middle_part
    branch_grad = middle_grad.astype(BF16)
    head_grads = exchange_tensor(
        [dot_right(branch_grad, w_out[d]).astype(BF16) for d in range(devices)]
    )
    mixed_grad = dot_left(deal, jnp.concatenate(head_grads, axis=0)).astype(BF16)
    out_grad = jnp.stack([dot_left(heads[d], branch_grad) for d in range(devices)])
    dqkv, drel = attend_back(qkv, rel, lse, mixed_grad)
    normed_parts = dot_right(dot(deal, dqkv).astype(BF16), w_qkv).astype(BF16)
    normed_parts = normed_parts.reshape(devices, -1, normed_parts.shape[1])
    normed_grad = sum_blocks(exchange_tensor([normed_parts[d] for d in range(devices)]))
    layer_part, attn_grad = norm_back(normed_grad, own_in, attn_gain)
    layer_grad = (middle_grad + layer_part).astype(BF16)
    every = jnp.concatenate(gather_tensor(layer_grad), axis=0)
    rows_out = dot_left(deal, every).astype(BF16)
    qkv_grad = dot_left(normed, dqkv)
    rel_grad = jnp.sum(drel, axis=-1).T
    small = jnp.concatenate([attn_grad[None], ffn_grad[None], router_grad.T], axis=0)
    return (rows_out, (qkv_grad, out_grad, small, rel_grad, in_grad, back_grad))


def body(
    x_in,
    cotangent,
    attn_gain,
    ffn_gain,
    w_query,
    w_key,
    w_value,
    w_out,
    rel_bias,
    w_router,
    w_in,
    w_back,
    routes,
    keep_mask,
):
    core = lax.axis_index("section")
    first = core == 0
    groups = lax.axis_size("expert")
    devices = lax.axis_size("tensor")
    experts = w_router.shape[2]
    tokens = x_in.shape[1]
    width = x_in.shape[2]
    capacity = 3 * tokens // (2 * experts)

    def both(own):
        other = swap_section(own)
        return (jnp.where(first, own, other), jnp.where(first, other, own))

    def pick(stack, index):
        return lax.dynamic_index_in_dim(stack, index, 0, keepdims=False)

    qkv_pair = both(jnp.concatenate([w_query[0], w_key[0], w_value[0]], axis=1))
    rel_pair = both(rel_bias[0])
    attn_pair = both(attn_gain)
    ffn_pair = both(ffn_gain)
    router_pair = both(w_router[0])
    out_pair = both(jnp.stack(gather_tensor(w_out[0])))
    in_all = lax.all_gather(w_in[0], "section", axis=0)
    back_all = lax.all_gather(w_back[0], "section", axis=0)
    own_ints = jnp.stack([pick(routes[0], core)[:, 0], pick(keep_mask[0], core)])
    sent_ints = jnp.stack([pick(routes[0], 1 - core)[:, 0], pick(keep_mask[0], 1 - core)])
    got_ints = swap_section(sent_ints)
    ints_pair = (jnp.where(first, own_ints, got_ints), jnp.where(first, got_ints, own_ints))

    weights, rels, plans = [], [], []
    for s in range(2):
        weights.append(
            (
                attn_pair[s][0].astype(F32),
                ffn_pair[s][0].astype(F32),
                qkv_pair[s],
                out_pair[s],
                router_pair[s],
                in_all[s],
                back_all[s],
            )
        )
        rels.append(rel_pair[s].astype(F32))
        plans.append(make_plan(ints_pair[s][0], ints_pair[s][1], experts, capacity))

    rows = pick(x_in, core)
    acts, saved = [], []
    for s in range(2):
        rows, kept = layer_forward(rows, weights[s], rels[s], plans[s])
        acts.append(rows)
        saved.append(kept)
    grads = [None, None]
    row_grads = [None, None]
    rows = pick(cotangent, core)
    for s in (1, 0):
        rows, grads[s] = layer_backward(saved[s], rows, weights[s], rels[s], plans[s])
        row_grads[s] = rows

    def whole_rows(pair):
        own = jnp.where(first, pair[0], pair[1])
        got = swap_section(jnp.where(first, pair[1], pair[0]))
        return jnp.stack([jnp.where(first, own, got), jnp.where(first, got, own)])[None]

    def whole_grad(number):
        low, high = grads[0][number], grads[1][number]
        got = swap_section(jnp.where(first, high, low).astype(BF16))
        return jnp.where(first, low, high) + got.astype(F32)

    qkv_grad, out_grad, small, rel_grad, in_grad, back_grad = [whole_grad(n) for n in range(6)]
    tall = jnp.concatenate(
        [out_grad, jnp.broadcast_to(small[None], (devices,) + small.shape)], axis=1
    ).astype(BF16)
    tall = sum_blocks(exchange_tensor([tall[d] for d in range(devices)]))
    wide = jnp.concatenate([qkv_grad, tall.T], axis=1)
    rel_wide = jnp.pad(rel_grad, ((0, 0), (0, wide.shape[1] - rel_grad.shape[1])))
    packed = jnp.concatenate(
        [wide.reshape(groups, -1, wide.shape[1]), rel_wide.reshape(groups, -1, wide.shape[1])],
        axis=1,
    ).astype(BF16)
    shares = jnp.sum(swap_experts(packed).astype(F32), axis=0)
    mine = width // groups
    cols = w_query.shape[2]
    return (
        whole_rows(acts),
        whole_rows(row_grads),
        shares[:mine, 4 * cols][None],
        shares[:mine, 4 * cols + 1][None],
        shares[:mine, :cols][None],
        shares[:mine, cols : 2 * cols][None],
        shares[:mine, 2 * cols : 3 * cols][None],
        shares[:mine, 3 * cols : 4 * cols].T[None],
        shares[mine:, : rel_bias.shape[2]][None],
        shares[:mine, 4 * cols + 2 :][None],
        in_grad[None],
        back_grad[None],
    )


def solution(mesh):
    placed = (
        P(None, "expert", None),
        P(None, "expert", None),
        P("section", None),
        P("section", None),
        P("section", None, "tensor"),
        P("section", None, "tensor"),
        P("section", None, "tensor"),
        P("section", "tensor", None),
        P("section", None, "tensor"),
        P("section", None, None),
        P("section", "expert", None, "tensor"),
        P("section", "expert", "tensor", None),
        P("section", None, "expert", None),
        P("section", None, "expert"),
    )
    return jax.shard_map(
        body,
        mesh=mesh,
        in_specs=placed,
        out_specs=(
            P("section", None, "expert", None),
            P("section", None, "expert", None),
            P("section", "expert"),
            P("section", "expert"),
            P("section", "expert", "tensor"),
            P("section", "expert", "tensor"),
            P("section", "expert", "tensor"),
            P("section", "tensor", "expert"),
            P("section", "expert", "tensor"),
            P("section", "expert", None),
            P("section", "expert", None, "tensor"),
            P("section", "expert", "tensor", None),
        ),
        check_vma=False,
    )
```

time: 4580 us -> 792 us (0.17)
  other arithmetic: 1550 us -> 53.9 us
  local copies, waits for them, and re-layouts: 1140 us -> 33.8 us
  blocking collectives: 662 us -> 55.5 us
  waiting for transfers between devices: 783 us -> 349 us
  matrix products: 368 us -> 147 us
  starting transfers between devices: 50.2 us -> 99.7 us
    scatter-add x1 -> x0, other arithmetic: 1390 us -> none  [make_bias(): return table_rows[:, index_grid]]
    gather x2 -> x0, local copies, waits for them, and re-layouts: 930 us -> none  [make_bias(): return table_rows[:, index_grid]]
    psum x3 -> x0, blocking collectives: 477 us -> none  [layer_forward(): expert_out = lax.psum(partial_out, 'tensor').astype(jnp.bfloat16)]
    psum x8 -> x0, waiting for transfers between devices: 409 us -> none  [the longest x3 192 us: layer_backward(): input_low = lax.psum(input_part.astype(jnp.bfloat16), 'tensor')]
    all_to_all x9 -> x6, waiting for transfers between devices: 360 us -> 60.5 us  [swap_experts(): lax.all_to_all(block, 'expert', split_axis=0, concat_axis=0, tiled=True)]
    ppermute x4 -> x75, waiting for transfers between devices: 2.46 us -> 287 us  [the longest x60 286 us: swap_tensor(): lax.ppermute(block, 'tensor', [(i, i ^ distance) for i in range(devices)])]
    dot_general x98 -> x70, matrix products: 368 us -> 147 us  [the longest x12 76.1 us: per_expert(): lax.dot_general(left, right, ((contract[:1], contract[1:]), ((0,), (0,)))...]
    all_to_all x3, blocking collectives: 176 us -> 55.5 us  [swap_experts(): lax.all_to_all(block, 'expert', split_axis=0, concat_axis=0, tiled=True)]
  transfers between devices with their start and end apart: 27 -> 83, of which waited for: 18 -> 54; matrix products, arithmetic and copies ran while one was open for 38% -> 20% of each run, Pallas kernels for 0% -> 2%
where the time goes in v1:
time: 792 us; the launch traced here: 782 us
  waiting for transfers between devices  349 us (44%)
  matrix products  147 us (19%)
  starting transfers between devices  99.7 us (13%)
  blocking collectives  55.5 us (7%)
  other arithmetic  53.9 us (7%)
  local copies, waits for them, and re-layouts  33.8 us (4%)
  Pallas kernels  27.2 us (3%)
  between operations  16.9 us (2%)
    ppermute x60, waiting for transfers between devices, swap_tensor(): lax.ppermute(block, 'tensor', [(i, i ^ distance) for i in range(devices)])  286 us
    dot_general x12, matrix products, per_expert(): lax.dot_general(left, right, ((contract[:1], contract[1:]), ((0,), (0,)))...  76.1 us
    ppermute x60, starting transfers between devices, swap_tensor(): lax.ppermute(block, 'tensor', [(i, i ^ distance) for i in range(devices)])  70.7 us
    all_to_all x6, waiting for transfers between devices, swap_experts(): lax.all_to_all(block, 'expert', split_axis=0, concat_axis=0, tiled=True)  60.5 us
    all_to_all x3, blocking collectives, swap_experts(): lax.all_to_all(block, 'expert', split_axis=0, concat_axis=0, tiled=True)  55.5 us
    dot_general x22, matrix products, dot_left(): lax.dot_general(left, right, (((0,), (0,)), ((), ())), preferred_element_...  37.4 us
    all_to_all x6, starting transfers between devices, swap_experts(): lax.all_to_all(block, 'expert', split_axis=0, concat_axis=0, tiled=True)  25.2 us
    unnamed x301, local copies, waits for them, and re-layouts  21.6 us
  transfers between devices with their start and end apart: 83, of which 54 were waited for; matrix products, arithmetic and copies ran while one was open for 20% of the time, Pallas kernels for 2%

profile of v1, /device:TPU:0, one launch (start us, length us, event | category | flops | bytes accessed | tf_op | source)
XLA Modules:
  0.0 782.4 jit_solution(1014284060034405839)
XLA Ops:
  49.1 20.4 %all_to_all.45 = bf16[4,96,768]{2,1,0:T(8,128)(2,1)S(1)} all-to-all(bf16[4,96,768]{2,1,0:T(8,128)(2,1)S(1)} %bitcast.314), channel_id=1, replica_groups=mesh['section'=2,'expert'=4,'tensor'=4] {'expert'}, dimensions={0} | all-to-all | bytes 1179648 | tf_op jit(solution)/shard_map/all_to_all | solution.py:251
  73.1 13.7 %collective-permute-done.15 = bf16[4,96,768]{2,1,0:T(8,128)(2,1)S(1)} collective-permute-done((bf16[4,96,768]{2,1,0:T(8,128)(2,1)S(1)}, bf16[4,96,768]{2,1,0:T(8,128)(2,1)S(1)}, u32[]{:S(2)}, u32[]{:S(2)}) %collective-permute-start.15) | collective-permute-done | bytes 589856 | tf_op jit(solution)/shard_map/ppermute | solution.py:235
  86.8 10.4 %collective-permute-done.14 = bf16[4,96,768]{2,1,0:T(8,128)(2,1)S(1)} collective-permute-done((bf16[4,96,768]{2,1,0:T(8,128)(2,1)S(1)}, bf16[4,96,768]{2,1,0:T(8,128)(2,1)S(1)}, u32[]{:S(2)}, u32[]{:S(2)}) %collective-permute-start.14) | collective-permute-done | bytes 589856 | tf_op jit(solution)/shard_map/ppermute | solution.py:235
  114.5 12.7 %collective-permute-done.16 = bf16[4,96,768]{2,1,0:T(8,128)(2,1)S(1)} collective-permute-done((bf16[4,96,768]{2,1,0:T(8,128)(2,1)S(1)}, bf16[4,96,768]{2,1,0:T(8,128)(2,1)S(1)}, u32[]{:S(2)}, u32[]{:S(2)}) %collective-permute-start.16) | collective-permute-done | bytes 589856 | tf_op jit(solution)/shard_map/ppermute | solution.py:235
  127.2 11.9 %collective-permute-done.18 = bf16[4,96,768]{2,1,0:T(8,128)(2,1)S(1)} collective-permute-done((bf16[4,96,768]{2,1,0:T(8,128)(2,1)S(1)}, bf16[4,96,768]{2,1,0:T(8,128)(2,1)S(1)}, u32[]{:S(2)}, u32[]{:S(2)}) %collective-permute-start.18) | collective-permute-done | bytes 589856 | tf_op jit(solution)/shard_map/ppermute | solution.py:235
  148.4 11.6 %all-to-all-done.1 = bf16[4,96,768]{2,1,0:T(8,128)(2,1)} async-done(((bf16[4,96,768]{2,1,0:T(8,128)(2,1)}), bf16[4,96,768]{2,1,0:T(8,128)(2,1)}, u32[]{:S(2)}, u32[]{:S(2)}) %all-to-all-start.1) | async-done | bytes 589856 | tf_op jit(solution)/shard_map/all_to_all | solution.py:251
  204.6 18.1 %all_to_all.46 = bf16[4,96,768]{2,1,0:T(8,128)(2,1)S(1)} all-to-all(bf16[4,96,768]{2,1,0:T(8,128)(2,1)S(1)} %bitcast.315), channel_id=1, replica_groups=mesh['section'=2,'expert'=4,'tensor'=4] {'expert'}, dimensions={0} | all-to-all | bytes 1179648 | tf_op jit(solution)/shard_map/all_to_all | solution.py:251
  226.3 13.7 %collective-permute-done.27 = bf16[4,96,768]{2,1,0:T(8,128)(2,1)S(1)} collective-permute-done((bf16[4,96,768]{2,1,0:T(8,128)(2,1)S(1)}, bf16[4,96,768]{2,1,0:T(8,128)(2,1)S(1)}, u32[]{:S(2)}, u32[]{:S(2)}) %collective-permute-start.27) | collective-permute-done | bytes 589856 | tf_op jit(solution)/shard_map/ppermute | solution.py:235
  240.0 10.4 %collective-permute-done.26 = bf16[4,96,768]{2,1,0:T(8,128)(2,1)S(1)} collective-permute-done((bf16[4,96,768]{2,1,0:T(8,128)(2,1)S(1)}, bf16[4,96,768]{2,1,0:T(8,128)(2,1)S(1)}, u32[]{:S(2)}, u32[]{:S(2)}) %collective-permute-start.26) | collective-permute-done | bytes 589856 | tf_op jit(solution)/shard_map/ppermute | solution.py:235
  263.4 12.7 %collective-permute-done.28 = bf16[4,96,768]{2,1,0:T(8,128)(2,1)S(1)} collective-permute-done((bf16[4,96,768]{2,1,0:T(8,128)(2,1)S(1)}, bf16[4,96,768]{2,1,0:T(8,128)(2,1)S(1)}, u32[]{:S(2)}, u32[]{:S(2)}) %collective-permute-start.28) | collective-permute-done | bytes 589856 | tf_op jit(solution)/shard_map/ppermute | solution.py:235
  276.1 11.4 %collective-permute-done.30 = bf16[4,96,768]{2,1,0:T(8,128)(2,1)S(1)} collective-permute-done((bf16[4,96,768]{2,1,0:T(8,128)(2,1)S(1)}, bf16[4,96,768]{2,1,0:T(8,128)(2,1)S(1)}, u32[]{:S(2)}, u32[]{:S(2)}) %collective-permute-start.30) | collective-permute-done | bytes 589856 | tf_op jit(solution)/shard_map/ppermute | solution.py:235
  295.7 12.1 %all-to-all-done.3 = bf16[4,96,768]{2,1,0:T(8,128)(2,1)} async-done(((bf16[4,96,768]{2,1,0:T(8,128)(2,1)}), bf16[4,96,768]{2,1,0:T(8,128)(2,1)}, u32[]{:S(2)}, u32[]{:S(2)}) %all-to-all-start.3) | async-done | bytes 589856 | tf_op jit(solution)/shard_map/all_to_all | solution.py:251
  312.0 17.0 %all_to_all.47 = bf16[4,96,768]{2,1,0:T(8,128)(2,1)S(1)} all-to-all(bf16[4,96,768]{2,1,0:T(8,128)(2,1)S(1)} %bitcast.316), channel_id=1, replica_groups=mesh['section'=2,'expert'=4,'tensor'=4] {'expert'}, dimensions={0} | all-to-all | bytes 1179648 | tf_op jit(solution)/shard_map/all_to_all | solution.py:251
  333.2 13.1 %collective-permute-done.37 = bf16[4,96,768]{2,1,0:T(8,128)(2,1)S(1)} collective-permute-done((bf16[4,96,768]{2,1,0:T(8,128)(2,1)S(1)}, bf16[4,96,768]{2,1,0:T(8,128)(2,1)S(1)}, u32[]{:S(2)}, u32[]{:S(2)}) %collective-permute-start.37) | collective-permute-done | bytes 589856 | tf_op jit(solution)/shard_map/ppermute | solution.py:235
  346.3 10.0 %collective-permute-done.36 = bf16[4,96,768]{2,1,0:T(8,128)(2,1)S(1)} collective-permute-done((bf16[4,96,768]{2,1,0:T(8,128)(2,1)S(1)}, bf16[4,96,768]{2,1,0:T(8,128)(2,1)S(1)}, u32[]{:S(2)}, u32[]{:S(2)}) %collective-permute-start.36) | collective-permute-done | bytes 589856 | tf_op jit(solution)/shard_map/ppermute | solution.py:235
  368.9 12.7 %collective-permute-done.38 = bf16[4,96,768]{2,1,0:T(8,128)(2,1)S(1)} collective-permute-done((bf16[4,96,768]{2,1,0:T(8,128)(2,1)S(1)}, bf16[4,96,768]{2,1,0:T(8,128)(2,1)S(1)}, u32[]{:S(2)}, u32[]{:S(2)}) %collective-permute-start.38) | collective-permute-done | bytes 589856 | tf_op jit(solution)/shard_map/ppermute | solution.py:235
  381.6 12.8 %collective-permute-done.40 = bf16[4,96,768]{2,1,0:T(8,128)(2,1)S(1)} collective-permute-done((bf16[4,96,768]{2,1,0:T(8,128)(2,1)S(1)}, bf16[4,96,768]{2,1,0:T(8,128)(2,1)S(1)}, u32[]{:S(2)}, u32[]{:S(2)}) %collective-permute-start.40) | collective-permute-done | bytes 589856 | tf_op jit(solution)/shard_map/ppermute | solution.py:235
  402.0 13.6 %all-to-all-done.5 = bf16[4,96,768]{2,1,0:T(8,128)(2,1)} async-done(((bf16[4,96,768]{2,1,0:T(8,128)(2,1)}), bf16[4,96,768]{2,1,0:T(8,128)(2,1)}, u32[]{:S(2)}, u32[]{:S(2)}) %all-to-all-start.5) | async-done | bytes 589856 | tf_op jit(solution)/shard_map/all_to_all | solution.py:251
  462.1 10.4 %collective-permute-done.45 = bf16[256,768]{1,0:T(8,128)(2,1)S(1)} collective-permute-done((bf16[256,768]{1,0:T(8,128)(2,1)S(1)}, bf16[256,768]{1,0:T(8,128)(2,1)S(1)}, u32[]{:S(2)}, u32[]{:S(2)}) %collective-permute-start.45) | collective-permute-done | bytes 393248 | tf_op jit(solution)/shard_map/ppermute | solution.py:235
  476.9 11.5 %collective-permute-done.32 = bf16[256,768]{1,0:T(8,128)(2,1)S(1)} collective-permute-done((bf16[256,768]{1,0:T(8,128)(2,1)S(1)}, bf16[256,768]{1,0:T(8,128)(2,1)S(1)}, u32[]{:S(2)}, u32[]{:S(2)}) %collective-permute-start.32) | collective-permute-done | bytes 393248 | tf_op jit(solution)/shard_map/ppermute | solution.py:235
  508.5 10.3 %all-to-all-done.6 = bf16[4,96,768]{2,1,0:T(8,128)(2,1)} async-done(((bf16[4,96,768]{2,1,0:T(8,128)(2,1)}), bf16[4,96,768]{2,1,0:T(8,128)(2,1)}, u32[]{:S(2)}, u32[]{:S(2)}) %all-to-all-start.6) | async-done | bytes 589856 | tf_op jit(solution)/shard_map/all_to_all | solution.py:251
  537.2 10.6 %collective-permute-done.51 = bf16[4,96,768]{2,1,0:T(8,128)(2,1)S(1)} collective-permute-done((bf16[4,96,768]{2,1,0:T(8,128)(2,1)S(1)}, bf16[4,96,768]{2,1,0:T(8,128)(2,1)S(1)}, u32[]{:S(2)}, u32[]{:S(2)}) %collective-permute-start.51) | collective-permute-done | bytes 589856 | tf_op jit(solution)/shard_map/ppermute | solution.py:235
  568.0 13.3 %select_convert_fusion = (bf16[4,768,768]{2,1,0:T(8,128)(2,1)}, f32[4,768,768]{2,1,0:T(8,128)}) fusion(f32[4,768,768]{2,1,0:T(8,128)S(1)} %fusion.166, pred[]{:T(512)S(6)} %eq.64, bf16[4,384,768]{2,1,0:T(8,128)(2,1)} %copy-done.62, bf16[4,96,768]{2,1,0:T(8,128)(2,1)} %copy-done.81, bf16[4,96,768]{2,1,0:T(8,128)(2,1)} %copy-done.82, ...), kind=kOutput, calls=%fused_computation.1 | convolution fusion | flops 1823735808 | bytes 28311552 | tf_op jit(solution)/shard_map/dot_general | solution.py:316
  597.5 10.1 %select_convert_fusion.1 = (bf16[4,768,768]{2,1,0:T(8,128)(2,1)}, f32[4,768,768]{2,1,0:T(8,128)}) fusion(f32[4,768,768]{2,1,0:T(8,128)} %fusion.169, pred[]{:T(512)S(6)} %eq.64, bf16[4,384,768]{2,1,0:T(8,128)(2,1)} %copy-done.63, bf16[4,96,768]{2,1,0:T(8,128)(2,1)} %copy-done.78, bf16[4,96,768]{2,1,0:T(8,128)(2,1)} %copy-done.79, ...), kind=kOutput, calls=%fused_computation.3 | convolution fusion | flops 1823735808 | bytes 28311552 | tf_op jit(solution)/shard_map/dot_general | solution.py:316
  (635 shorter events, 461.0 us)
Async XLA Ops:
  7.2 90.9 %all-gather.3.cloned.1.call-start = ((), (), s32[]{:S(2)}) async-start(), calls=%async_computation.9 | async-start | bytes 14155776 | tf_op jit(solution)/shard_map/all_gather | solution.py:443
  8.0 97.8 %all-gather.5.cloned.1.call-start = ((), (), s32[]{:S(2)}) async-start(), calls=%async_computation.10 | async-start | bytes 14155776 | tf_op jit(solution)/shard_map/all_gather | solution.py:444
  72.0 26.1 %collective-permute-start.13 = (bf16[4,96,768]{2,1,0:T(8,128)(2,1)S(1)}, bf16[4,96,768]{2,1,0:T(8,128)(2,1)}, u32[]{:S(2)}, u32[]{:S(2)}) collective-permute-start(bf16[4,96,768]{2,1,0:T(8,128)(2,1)S(1)} %bitcast.336), channel_id=1, source_target_pairs={{0,1},{1,0},{2,3},{3,2},{4,5},{5,4},{6,7},{7,6},{8,9},{9,8},{10,11... | collective-permute-start | bytes 1769480 | tf_op jit(solution)/shard_map/ppermute | solution.py:235
  111.9 27.3 %collective-permute-start.18 = (bf16[4,96,768]{2,1,0:T(8,128)(2,1)S(1)}, bf16[4,96,768]{2,1,0:T(8,128)(2,1)S(1)}, u32[]{:S(2)}, u32[]{:S(2)}) collective-permute-start(bf16[4,96,768]{2,1,0:T(8,128)(2,1)S(1)} %get-tuple-element.140), channel_id=1, source_target_pairs={{0,3},{1,2},{2,1},{3,0},{4,7},{5,6},{6,5},{7,4},{8,11},{9,10},{10,... | collective-permute-start | bytes 1769480 | tf_op jit(solution)/shard_map/ppermute | solution.py:235
  113.0 27.4 %collective-permute-start.17 = (bf16[4,96,768]{2,1,0:T(8,128)(2,1)S(1)}, bf16[4,96,768]{2,1,0:T(8,128)(2,1)S(1)}, u32[]{:S(2)}, u32[]{:S(2)}) collective-permute-start(bf16[4,96,768]{2,1,0:T(8,128)(2,1)S(1)} %get-tuple-element.141), channel_id=1, source_target_pairs={{0,2},{1,3},{2,0},{3,1},{4,6},{5,7},{6,4},{7,5},{8,10},{9,11},{10,... | collective-permute-start | bytes 1769480 | tf_op jit(solution)/shard_map/ppermute | solution.py:235
  224.1 26.3 %collective-permute-start.26 = (bf16[4,96,768]{2,1,0:T(8,128)(2,1)S(1)}, bf16[4,96,768]{2,1,0:T(8,128)(2,1)S(1)}, u32[]{:S(2)}, u32[]{:S(2)}) collective-permute-start(bf16[4,96,768]{2,1,0:T(8,128)(2,1)S(1)} %bitcast.322), channel_id=1, source_target_pairs={{0,2},{1,3},{2,0},{3,1},{4,6},{5,7},{6,4},{7,5},{8,10},{9,11},{10,... | collective-permute-start | bytes 1769480 | tf_op jit(solution)/shard_map/ppermute | solution.py:235
  260.4 27.1 %collective-permute-start.30 = (bf16[4,96,768]{2,1,0:T(8,128)(2,1)S(1)}, bf16[4,96,768]{2,1,0:T(8,128)(2,1)S(1)}, u32[]{:S(2)}, u32[]{:S(2)}) collective-permute-start(bf16[4,96,768]{2,1,0:T(8,128)(2,1)S(1)} %get-tuple-element.135), channel_id=1, source_target_pairs={{0,3},{1,2},{2,1},{3,0},{4,7},{5,6},{6,5},{7,4},{8,11},{9,10},{10,... | collective-permute-start | bytes 1769480 | tf_op jit(solution)/shard_map/ppermute | solution.py:235
  262.1 27.0 %collective-permute-start.29 = (bf16[4,96,768]{2,1,0:T(8,128)(2,1)S(1)}, bf16[4,96,768]{2,1,0:T(8,128)(2,1)S(1)}, u32[]{:S(2)}, u32[]{:S(2)}) collective-permute-start(bf16[4,96,768]{2,1,0:T(8,128)(2,1)S(1)} %get-tuple-element.136), channel_id=1, source_target_pairs={{0,2},{1,3},{2,0},{3,1},{4,6},{5,7},{6,4},{7,5},{8,10},{9,11},{10,... | collective-permute-start | bytes 1769480 | tf_op jit(solution)/shard_map/ppermute | solution.py:235
  366.8 27.6 %collective-permute-start.40 = (bf16[4,96,768]{2,1,0:T(8,128)(2,1)S(1)}, bf16[4,96,768]{2,1,0:T(8,128)(2,1)S(1)}, u32[]{:S(2)}, u32[]{:S(2)}) collective-permute-start(bf16[4,96,768]{2,1,0:T(8,128)(2,1)S(1)} %get-tuple-element.132), channel_id=1, source_target_pairs={{0,3},{1,2},{2,1},{3,0},{4,7},{5,6},{6,5},{7,4},{8,11},{9,10},{10,... | collective-permute-start | bytes 1769480 | tf_op jit(solution)/shard_map/ppermute | solution.py:235
  368.5 27.3 %collective-permute-start.39 = (bf16[4,96,768]{2,1,0:T(8,128)(2,1)S(1)}, bf16[4,96,768]{2,1,0:T(8,128)(2,1)S(1)}, u32[]{:S(2)}, u32[]{:S(2)}) collective-permute-start(bf16[4,96,768]{2,1,0:T(8,128)(2,1)S(1)} %get-tuple-element.133), channel_id=1, source_target_pairs={{0,2},{1,3},{2,0},{3,1},{4,6},{5,7},{6,4},{7,5},{8,10},{9,11},{10,... | collective-permute-start | bytes 1769480 | tf_op jit(solution)/shard_map/ppermute | solution.py:235
  443.6 28.9 %collective-permute-start.45 = (bf16[256,768]{1,0:T(8,128)(2,1)S(1)}, bf16[256,768]{1,0:T(8,128)(2,1)S(1)}, u32[]{:S(2)}, u32[]{:S(2)}) collective-permute-start(bf16[256,768]{1,0:T(8,128)(2,1)S(1)} %get-tuple-element.147), channel_id=1, source_target_pairs={{0,2},{1,3},{2,0},{3,1},{4,6},{5,7},{6,4},{7,5},{8,10},{9,11},{10,... | collective-permute-start | bytes 1179656 | tf_op jit(solution)/shard_map/ppermute | solution.py:235
  445.3 31.3 %collective-permute-start.33 = (bf16[256,768]{1,0:T(8,128)(2,1)S(1)}, bf16[256,768]{1,0:T(8,128)(2,1)S(1)}, u32[]{:S(2)}, u32[]{:S(2)}) collective-permute-start(bf16[256,768]{1,0:T(8,128)(2,1)S(1)} %copy-done.85), channel_id=1, source_target_pairs={{0,3},{1,2},{2,1},{3,0},{4,7},{5,6},{6,5},{7,4},{8,11},{9,10},{10,... | collective-permute-start | bytes 1179656 | tf_op jit(solution)/shard_map/ppermute | solution.py:235
  446.9 41.4 %collective-permute-start.32 = (bf16[256,768]{1,0:T(8,128)(2,1)S(1)}, bf16[256,768]{1,0:T(8,128)(2,1)S(1)}, u32[]{:S(2)}, u32[]{:S(2)}) collective-permute-start(bf16[256,768]{1,0:T(8,128)(2,1)S(1)} %copy-done.85), channel_id=1, source_target_pairs={{0,2},{1,3},{2,0},{3,1},{4,6},{5,7},{6,4},{7,5},{8,10},{9,11},{10,... | collective-permute-start | bytes 1179656 | tf_op jit(solution)/shard_map/ppermute | solution.py:235
  453.7 34.7 %collective-permute-start.31 = (bf16[256,768]{1,0:T(8,128)(2,1)S(1)}, bf16[256,768]{1,0:T(8,128)(2,1)S(1)}, u32[]{:S(2)}, u32[]{:S(2)}) collective-permute-start(bf16[256,768]{1,0:T(8,128)(2,1)S(1)} %copy-done.85), channel_id=1, source_target_pairs={{0,1},{1,0},{2,3},{3,2},{4,5},{5,4},{6,7},{7,6},{8,9},{9,8},{10,11... | collective-permute-start | bytes 1179656 | tf_op jit(solution)/shard_map/ppermute | solution.py:235
  492.2 31.3 %collective-permute-start.34 = (bf16[1024,768]{0,1:T(8,128)(2,1)}, bf16[1024,768]{0,1:T(8,128)(2,1)}, u32[]{:S(2)}, u32[]{:S(2)}) collective-permute-start(bf16[1024,768]{0,1:T(8,128)(2,1)} %get-tuple-element.207), channel_id=1, source_target_pairs={{0,16},{16,0},{1,17},{17,1},{2,18},{18,2},{3,19},{19,3},{4,20},{20... | collective-permute-start | bytes 4718600 | tf_op jit(solution)/shard_map/ppermute | solution.py:247
  521.6 26.2 %collective-permute-start.51 = (bf16[4,96,768]{2,1,0:T(8,128)(2,1)S(1)}, bf16[4,96,768]{2,1,0:T(8,128)(2,1)S(1)}, u32[]{:S(2)}, u32[]{:S(2)}) collective-permute-start(bf16[4,96,768]{2,1,0:T(8,128)(2,1)S(1)} %bitcast.303), channel_id=1, source_target_pairs={{0,2},{1,3},{2,0},{3,1},{4,6},{5,7},{6,4},{7,5},{8,10},{9,11},{10,... | collective-permute-start | bytes 1769480 | tf_op jit(solution)/shard_map/ppermute | solution.py:235
  560.7 28.9 %collective-permute-start.53 = (bf16[4,96,768]{2,1,0:T(8,128)(2,1)}, bf16[4,96,768]{2,1,0:T(8,128)(2,1)}, u32[]{:S(2)}, u32[]{:S(2)}) collective-permute-start(bf16[4,96,768]{2,1,0:T(8,128)(2,1)} %get-tuple-element.128), channel_id=1, source_target_pairs={{0,1},{1,0},{2,3},{3,2},{4,5},{5,4},{6,7},{7,6},{8,9},{9,8},{10,11... | collective-permute-start | bytes 1769480 | tf_op jit(solution)/shard_map/ppermute | solution.py:235
  562.0 27.9 %collective-permute-start.55 = (bf16[4,96,768]{2,1,0:T(8,128)(2,1)}, bf16[4,96,768]{2,1,0:T(8,128)(2,1)}, u32[]{:S(2)}, u32[]{:S(2)}) collective-permute-start(bf16[4,96,768]{2,1,0:T(8,128)(2,1)} %get-tuple-element.129), channel_id=1, source_target_pairs={{0,3},{1,2},{2,1},{3,0},{4,7},{5,6},{6,5},{7,4},{8,11},{9,10},{10,... | collective-permute-start | bytes 1769480 | tf_op jit(solution)/shard_map/ppermute | solution.py:235
  563.7 27.4 %collective-permute-start.54 = (bf16[4,96,768]{2,1,0:T(8,128)(2,1)S(1)}, bf16[4,96,768]{2,1,0:T(8,128)(2,1)}, u32[]{:S(2)}, u32[]{:S(2)}) collective-permute-start(bf16[4,96,768]{2,1,0:T(8,128)(2,1)S(1)} %get-tuple-element.130), channel_id=1, source_target_pairs={{0,2},{1,3},{2,0},{3,1},{4,6},{5,7},{6,4},{7,5},{8,10},{9,11},{10,... | collective-permute-start | bytes 1769480 | tf_op jit(solution)/shard_map/ppermute | solution.py:235
  581.3 158.5 %collective-permute-start.74 = (bf16[4,768,768]{2,1,0:T(8,128)(2,1)}, bf16[4,768,768]{2,1,0:T(8,128)(2,1)}, u32[]{:S(2)}, u32[]{:S(2)}) collective-permute-start(bf16[4,768,768]{2,1,0:T(8,128)(2,1)} %get-tuple-element.222), channel_id=1, source_target_pairs={{0,16},{16,0},{1,17},{17,1},{2,18},{18,2},{3,19},{19,3},{4,20},{20... | collective-permute-start | bytes 14155784 | tf_op jit(solution)/shard_map/ppermute | solution.py:247
  607.6 141.2 %collective-permute-start.73 = (bf16[4,768,768]{2,1,0:T(8,128)(2,1)}, bf16[4,768,768]{2,1,0:T(8,128)(2,1)}, u32[]{:S(2)}, u32[]{:S(2)}) collective-permute-start(bf16[4,768,768]{2,1,0:T(8,128)(2,1)} %get-tuple-element.220), channel_id=1, source_target_pairs={{0,16},{16,0},{1,17},{17,1},{2,18},{18,2},{3,19},{19,3},{4,20},{20... | collective-permute-start | bytes 14155784 | tf_op jit(solution)/shard_map/ppermute | solution.py:247
  660.6 38.6 %collective-permute-start.67 = (bf16[4,192,768]{2,1,0:T(8,128)(2,1)}, bf16[4,192,768]{2,1,0:T(8,128)(2,1)}, u32[]{:S(2)}, u32[]{:S(2)}) collective-permute-start(bf16[4,192,768]{2,1,0:T(8,128)(2,1)} %select_convert_fusion.2), channel_id=1, source_target_pairs={{0,16},{16,0},{1,17},{17,1},{2,18},{18,2},{3,19},{19,3},{4,20},{20... | collective-permute-start | bytes 3538952 | tf_op jit(solution)/shard_map/ppermute | solution.py:247
  699.3 35.8 %collective-permute-start.65 = (bf16[1024,768]{0,1:T(8,128)(2,1)}, bf16[1024,768]{0,1:T(8,128)(2,1)}, u32[]{:S(2)}, u32[]{:S(2)}) collective-permute-start(bf16[1024,768]{0,1:T(8,128)(2,1)} %get-tuple-element.216), channel_id=1, source_target_pairs={{0,16},{16,0},{1,17},{17,1},{2,18},{18,2},{3,19},{19,3},{4,20},{20... | collective-permute-start | bytes 4718600 | tf_op jit(solution)/shard_map/ppermute | solution.py:247
  730.6 39.0 %all-to-all-start.8 = ((bf16[4,200,786]{2,1,0:T(8,128)(2,1)}), bf16[4,200,786]{2,1,0:T(8,128)(2,1)}, u32[]{:S(2)}, u32[]{:S(2)}) async-start(bf16[4,200,786]{2,1,0:T(8,128)(2,1)} %pad_maximum_fusion.6), calls=%async_computation.8 | async-start | bytes 2867200 | tf_op jit(solution)/shard_map/all_to_all | solution.py:251
  (206 other events, 3705.3 us)
Sparse Core Ops, SparseCore 0:
  9.6 26.2 all-gather.2
  37.4 23.0 all-gather.4

commit v2 on v1

--- a/solution.py
+++ b/solution.py
@@ -258,6 +258,10 @@
     return total
 
 
+def chunks_of(local):
+    return 2 if local % 2 == 0 else 1
+
+
 def make_plan(route_rows, keep_rows, experts, capacity):
     tokens = route_rows.shape[0]
     devices = lax.axis_size("tensor")
@@ -284,19 +288,38 @@
     first = (starts.astype(jnp.int32) - rank + devices - 1) // devices
     slot = rows - jnp.sum(jnp.where(chosen_own, first[None, :], 0), axis=1, dtype=jnp.int32)
     slot = jnp.where(keep_own > 0, route_own * share + slot, -1)
-    place = (jnp.arange(experts * share, dtype=jnp.int32)[:, None] == slot[None, :]).astype(BF16)
-    return (deal, deal[:owned], place, chosen_own.astype(F32), keep_own.astype(F32))
-
-
-def to_experts(rows, place, local):
     groups = lax.axis_size("expert")
-    width = rows.shape[1]
-    sent = dot(place, rows).astype(BF16).reshape(groups, -1, width)
-    got = swap_experts(sent)
-    share = got.shape[1] // local
-    got = got.reshape(groups, local, share, width).transpose(1, 0, 2, 3)
-    got = got.reshape(local, groups * share, width)
+    local = experts // groups
+    chunks = chunks_of(local)
+    ahead = (lax.axis_index("expert") + jnp.arange(groups, dtype=jnp.int32)) % groups
+    inner = np.arange(local * share, dtype=np.int32).reshape(chunks, -1)
+    places = []
+    for chunk in inner:
+        wanted_slot = (ahead[:, None] * (local * share) + chunk[None, :]).reshape(-1)
+        places.append((wanted_slot[:, None] == slot[None, :]).astype(BF16))
+    return (deal, deal[:owned], places, chosen_own.astype(F32), keep_own.astype(F32))
+
+
+def shift_experts(block, distance):
+    groups = lax.axis_size("expert")
+    if distance % groups == 0:
+        return block
+    return lax.ppermute(block, "expert", [(i, (i + distance) % groups) for i in range(groups)])
+
+
+def to_groups(rows, local):
+    groups = lax.axis_size("expert")
+    rows = rows.reshape(groups, local, -1, rows.shape[1])
+    return jnp.concatenate([shift_experts(rows[d], d) for d in range(groups)], axis=1)
+
+
+def all_shares(got):
     return jnp.concatenate(gather_tensor(got), axis=1)
+
+
+def send_tokens(rows, places, local):
+    per_chunk = local // len(places)
+    return [to_groups(dot(place, rows).astype(BF16), per_chunk) for place in places]
 
 
 def from_experts(parts, place):
@@ -307,9 +330,12 @@
     parts = parts.astype(BF16)
     blocks = exchange_tensor([parts[:, d * own : (d + 1) * own] for d in range(devices)])
     summed = sum_blocks(blocks).astype(BF16)
-    summed = summed.reshape(local, groups, own // groups, width).transpose(1, 0, 2, 3)
-    back = swap_experts(summed.reshape(groups, -1, width)).reshape(-1, width)
-    return dot_left(place, back)
+    share = own // groups
+    back = [
+        shift_experts(summed[:, d * share : (d + 1) * share].reshape(-1, width), -d)
+        for d in range(groups)
+    ]
+    return dot_left(place, jnp.concatenate(back, axis=0))
 
 
 def per_expert(left, right, contract):
@@ -318,16 +344,70 @@
     )
 
 
-def layer_forward(rows_in, weights, rel, plan):
+def grads_kernel(pick_ref, *refs, chunks, per_chunk):
+    lefts, rights = refs[: 2 * chunks], refs[2 * chunks : 4 * chunks]
+    extra, out_ref = refs[4 * chunks : -1], refs[-1]
+    expert = pl.program_id(0)
+    for layer in range(2):
+        for c in range(chunks):
+
+            @pl.when((pick_ref[0] == layer) & (expert // per_chunk == c))
+            def _():
+                value = dot_left(lefts[layer * chunks + c][0], rights[layer * chunks + c][0])
+                for ref in extra:
+                    value = value + ref[0].astype(F32)
+                out_ref[0] = value.astype(out_ref.dtype)
+
+
+def expert_grads(lefts, rights, layer, extra, kind):
+    chunks = len(lefts[0])
+    per_chunk, slots, rows = lefts[0][0].shape
+    cols = rights[0][0].shape[2]
+    local = chunks * per_chunk
+
+    def spec(owner, c, width):
+        def place(e, pick):
+            own = jnp.clip(e - c * per_chunk, 0, per_chunk - 1)
+            return (jnp.where(pick[0] == owner, own, 0), 0, 0)
+
+        return pl.BlockSpec((1, slots, width), place)
+
+    whole = pl.BlockSpec((1, rows, cols), lambda e, pick: (e, 0, 0))
+    names = [(owner, c) for owner in range(2) for c in range(chunks)]
+    return pl.pallas_call(
+        functools.partial(grads_kernel, chunks=chunks, per_chunk=per_chunk),
+        grid_spec=pltpu.PrefetchScalarGridSpec(
+            num_scalar_prefetch=1,
+            grid=(local,),
+            in_specs=[spec(owner, c, rows) for owner, c in names]
+            + [spec(owner, c, cols) for owner, c in names]
+            + [whole] * len(extra),
+            out_specs=whole,
+        ),
+        out_shape=jax.ShapeDtypeStruct((local, rows, cols), kind),
+        compiler_params=pltpu.CompilerParams(
+            dimension_semantics=("arbitrary",), vmem_limit_bytes=40 << 20
+        ),
+        cost_estimate=pl.CostEstimate(
+            flops=2 * local * slots * rows * cols,
+            transcendentals=0,
+            bytes_accessed=local * (6 * rows * cols + 2 * slots * (rows + cols)),
+        ),
+    )(layer, *lefts[0], *lefts[1], *rights[0], *rights[1], *extra)
+
+
+def layer_forward(rows_in, weights, rel, plan, ahead, with_gates):
     attn_gain, ffn_gain, w_qkv, w_out, w_router, w_in, w_back = weights
-    deal, deal_own, place, chosen, kept = plan
+    deal, deal_own, places, chosen, kept = plan
     devices = lax.axis_size("tensor")
-    local = w_in.shape[0]
+    local = sum(block.shape[0] for block in w_in)
     layer_in = rows_in.astype(F32)
     scale_one = root_mean(layer_in)
     normed = (layer_in * scale_one * attn_gain).astype(BF16)
     qkv = dot(normed, w_qkv).astype(BF16)
     mixed, lse = attend(qkv, rel)
+    if with_gates:
+        mixed, ahead = lax.optimization_barrier((mixed, ahead))
     cols = mixed.shape[1]
     dealt = dot(deal, mixed).astype(BF16).reshape(devices, -1, cols)
     heads = exchange_tensor([dealt[d] for d in range(devices)])
@@ -338,18 +418,26 @@
     normed_two = (middle * scale_two * ffn_gain).astype(BF16)
     probs = jax.nn.softmax(dot(normed_two, w_router), axis=-1)
     gate = jnp.sum(probs * chosen, axis=-1)
-    incoming = to_experts(normed_two, place, local)
-    inner = per_expert(incoming, w_in, (2, 1))
-    cumulative = 0.5 * (1.0 + lax.erf(inner * np.float32(np.sqrt(0.5))))
-    density = jnp.exp(-0.5 * inner * inner) * np.float32(1.0 / np.sqrt(2.0 * np.pi))
-    hidden = (inner * cumulative).astype(BF16)
-    slope = (cumulative + inner * density).astype(BF16)
-    per_token = from_experts(per_expert(hidden, w_back, (2, 1)), place)
+    gates = send_gates(kept * gate, places, local) if with_gates else None
+    incoming = [all_shares(got) for got in send_tokens(normed_two, places, local)]
+    if not with_gates:
+        incoming[-1], ahead = lax.optimization_barrier((incoming[-1], ahead))
+    hidden, slope, per_token = [], [], 0.0
+    for place, rows, first, second in zip(places, incoming, w_in, w_back):
+        inner = per_expert(rows, first, (2, 1))
+        cumulative = 0.5 * (1.0 + lax.erf(inner * np.float32(np.sqrt(0.5))))
+        density = jnp.exp(-0.5 * inner * inner) * np.float32(1.0 / np.sqrt(2.0 * np.pi))
+        hidden.append((inner * cumulative).astype(BF16))
+        slope.append((cumulative + inner * density).astype(BF16))
+        parts = per_expert(hidden[-1], second, (2, 1)).astype(BF16)
+        if with_gates:
+            parts, gates = lax.optimization_barrier((parts, gates))
+        per_token = per_token + from_experts(parts, place)
     output = (middle + (kept * gate)[:, None] * per_token).astype(BF16)
     every = jnp.concatenate(gather_tensor(output), axis=0)
     rows_out = dot_left(deal, every).astype(BF16)
     saved = (own_in, normed, qkv, lse, heads, middle, normed_two, probs, gate)
-    return (rows_out, saved + (incoming, hidden, slope, per_token))
+    return (rows_out, saved + (incoming, hidden, slope, per_token), ahead, gates)
 
 
 def norm_back(grad, values, gain):
@@ -361,22 +449,39 @@
     return (values_grad, jnp.sum(grad * values * scale, axis=0))
 
 
-def layer_backward(saved, rows_grad, weights, rel, plan):
+def send_gates(gates, places, local):
+    groups = lax.axis_size("expert")
+    factors = [
+        jnp.sum(place.astype(F32) * gates[None, :], axis=1).reshape(groups, local // len(places), -1)
+        for place in places
+    ]
+    factors = jnp.concatenate(factors, axis=1)
+    got = jnp.concatenate([shift_experts(factors[d], d) for d in range(groups)], axis=1)
+    return jnp.split(all_shares(got)[:, :, None], len(places))
+
+
+def layer_backward(saved, rows_grad, weights, rel, plan, early, gates, finish):
     attn_gain, ffn_gain, w_qkv, w_out, w_router, w_in, w_back = weights
-    deal, deal_own, place, chosen, kept = plan
+    deal, deal_own, places, chosen, kept = plan
     own_in, normed, qkv, lse, heads, middle, normed_two, probs, gate = saved[:9]
     incoming, hidden, slope, per_token = saved[9:]
     devices = lax.axis_size("tensor")
-    local = w_in.shape[0]
+    local = sum(block.shape[0] for block in w_in)
     grad_out = dot(deal_own, rows_grad)
     gated = ((kept * gate)[:, None] * grad_out).astype(BF16)
     gate_grad = kept * jnp.sum(grad_out * per_token, axis=-1)
-    expert_grad = to_experts(gated, place, local)
-    hidden_grad = per_expert(expert_grad, w_back, (2, 2))
-    inner_grad = (hidden_grad * slope.astype(F32)).astype(BF16)
-    input_rows = from_experts(per_expert(inner_grad, w_in, (2, 2)), place)
-    back_grad = per_expert(hidden, expert_grad, (1, 1))
-    in_grad = per_expert(incoming, inner_grad, (1, 1))
+    if early is None:
+        expert_grad = [all_shares(got) for got in send_tokens(gated, places, local)]
+    else:
+        expert_grad = [
+            (factor * rows.astype(F32)).astype(BF16) for factor, rows in zip(gates, early)
+        ]
+    input_rows, inner_grads = 0.0, []
+    for n, place in enumerate(places):
+        hidden_grad = per_expert(expert_grad[n], w_back[n], (2, 2))
+        inner_grad = (hidden_grad * slope[n].astype(F32)).astype(BF16)
+        input_rows = input_rows + from_experts(per_expert(inner_grad, w_in[n], (2, 2)), place)
+        inner_grads.append(inner_grad)
     logit_grad = (probs * (chosen - gate[:, None]) * gate_grad[:, None]).astype(BF16)
     router_grad = dot_left(normed_two, logit_grad)
     normed_two_grad = input_rows + dot_right(logit_grad, w_router)
@@ -388,18 +493,23 @@
     )
     mixed_grad = dot_left(deal, jnp.concatenate(head_grads, axis=0)).astype(BF16)
     out_grad = jnp.stack([dot_left(heads[d], branch_grad) for d in range(devices)])
+    small = jnp.concatenate([ffn_grad[None], router_grad.T], axis=0)
+    beside, fill = finish[0](inner_grads, expert_grad, out_grad, small)
     dqkv, drel = attend_back(qkv, rel, lse, mixed_grad)
+    dqkv, beside = lax.optimization_barrier((dqkv, beside))
+    qkv_grad = dot_left(normed, dqkv)
+    rel_grad = jnp.sum(drel, axis=-1).T
     normed_parts = dot_right(dot(deal, dqkv).astype(BF16), w_qkv).astype(BF16)
     normed_parts = normed_parts.reshape(devices, -1, normed_parts.shape[1])
-    normed_grad = sum_blocks(exchange_tensor([normed_parts[d] for d in range(devices)]))
+    blocks = exchange_tensor([normed_parts[d] for d in range(devices)])
+    blocks, fill = lax.optimization_barrier((blocks, fill))
+    normed_grad = sum_blocks(blocks)
     layer_part, attn_grad = norm_back(normed_grad, own_in, attn_gain)
     layer_grad = (middle_grad + layer_part).astype(BF16)
-    every = jnp.concatenate(gather_tensor(layer_grad), axis=0)
-    rows_out = dot_left(deal, every).astype(BF16)
-    qkv_grad = dot_left(normed, dqkv)
-    rel_grad = jnp.sum(drel, axis=-1).T
-    small = jnp.concatenate([attn_grad[None], ffn_grad[None], router_grad.T], axis=0)
-    return (rows_out, (qkv_grad, out_grad, small, rel_grad, in_grad, back_grad))
+    last = finish[1](qkv_grad, rel_grad, beside)
+    blocks, last = lax.optimization_barrier((gather_tensor(layer_grad), last))
+    rows_out = dot_left(deal, jnp.concatenate(blocks, axis=0)).astype(BF16)
+    return (rows_out, (attn_grad, fill, last))
 
 
 def body(
@@ -447,6 +557,7 @@
     got_ints = swap_section(sent_ints)
     ints_pair = (jnp.where(first, own_ints, got_ints), jnp.where(first, got_ints, own_ints))
 
+    chunks = chunks_of(w_in.shape[1])
     weights, rels, plans = [], [], []
     for s in range(2):
         weights.append(
@@ -456,61 +567,106 @@
                 qkv_pair[s],
                 out_pair[s],
                 router_pair[s],
-                in_all[s],
-                back_all[s],
+                jnp.split(in_all[s], chunks),
+                jnp.split(back_all[s], chunks),
             )
         )
         rels.append(rel_pair[s].astype(F32))
         plans.append(make_plan(ints_pair[s][0], ints_pair[s][1], experts, capacity))
 
+    ahead = send_tokens(
+        dot(plans[1][1], pick(cotangent, core)).astype(BF16), plans[1][2], w_in.shape[1]
+    )
     rows = pick(x_in, core)
     acts, saved = [], []
     for s in range(2):
-        rows, kept = layer_forward(rows, weights[s], rels[s], plans[s])
+        rows, kept, ahead, gates = layer_forward(rows, weights[s], rels[s], plans[s], ahead, s == 1)
+        if s == 0:
+            ahead = [all_shares(got) for got in ahead]
         acts.append(rows)
         saved.append(kept)
+    def whole_grad(low, high):
+        got = swap_section(jnp.where(first, high, low).astype(BF16))
+        return jnp.where(first, low, high) + got.astype(F32)
+
+    own_layer = core.reshape(1)
+    mine = width // groups
+    cols = w_query.shape[2]
+    held_experts, held_attention = [], []
+
+    def expert_part(inner_grads, expert_grad, out_grad, small):
+        held = held_experts
+        held.append((inner_grads, expert_grad, out_grad, small))
+        if len(held) < 2:
+            return ((out_grad, small), ())
+        in_pair = ([saved[s][9] for s in range(2)], [held[1 - s][0] for s in range(2)])
+        back_pair = ([saved[s][10] for s in range(2)], [held[1 - s][1] for s in range(2)])
+        in_got = swap_section(expert_grads(*in_pair, 1 - own_layer, [], BF16))
+        back_got = swap_section(expert_grads(*back_pair, 1 - own_layer, [], BF16))
+        in_grad = expert_grads(*in_pair, own_layer, [in_got], F32)
+        back_grad = expert_grads(*back_pair, own_layer, [back_got], F32)
+        out_sum = whole_grad(held[1][2], held[0][2])
+        small_sum = whole_grad(held[1][3], held[0][3])
+        tall = jnp.concatenate(
+            [out_sum, jnp.broadcast_to(small_sum[None], (devices,) + small_sum.shape)], axis=1
+        ).astype(BF16)
+        return (sum_blocks(exchange_tensor([tall[d] for d in range(devices)])), (in_grad, back_grad))
+
+    def attention_part(qkv_grad, rel_grad, tall):
+        held = held_attention
+        held.append((qkv_grad, rel_grad))
+        if len(held) < 2:
+            return ()
+        wide = jnp.concatenate([whole_grad(qkv_grad, held[0][0]), tall.T], axis=1)
+        rel_sum = whole_grad(rel_grad, held[0][1])
+        rel_wide = jnp.pad(rel_sum, ((0, 0), (0, wide.shape[1] - rel_sum.shape[1])))
+        packed = jnp.concatenate(
+            [wide.reshape(groups, -1, wide.shape[1]), rel_wide.reshape(groups, -1, wide.shape[1])],
+            axis=1,
+        ).astype(BF16)
+        shares = jnp.sum(swap_experts(packed).astype(F32), axis=0)
+        return (
+            shares[:mine, 4 * cols][None],
+            shares[:mine, :cols][None],
+            shares[:mine, cols : 2 * cols][None],
+            shares[:mine, 2 * cols : 3 * cols][None],
+            shares[:mine, 3 * cols : 4 * cols].T[None],
+            shares[mine:, : rel_bias.shape[2]][None],
+            shares[:mine, 4 * cols + 1 :][None],
+        )
+
     grads = [None, None]
     row_grads = [None, None]
     rows = pick(cotangent, core)
     for s in (1, 0):
-        rows, grads[s] = layer_backward(saved[s], rows, weights[s], rels[s], plans[s])
+        rows, grads[s] = layer_backward(
+            saved[s],
+            rows,
+            weights[s],
+            rels[s],
+            plans[s],
+            ahead if s == 1 else None,
+            gates,
+            (expert_part, attention_part),
+        )
         row_grads[s] = rows
 
     def whole_rows(pair):
         own = jnp.where(first, pair[0], pair[1])
         got = swap_section(jnp.where(first, pair[1], pair[0]))
-        return jnp.stack([jnp.where(first, own, got), jnp.where(first, got, own)])[None]
-
-    def whole_grad(number):
-        low, high = grads[0][number], grads[1][number]
-        got = swap_section(jnp.where(first, high, low).astype(BF16))
-        return jnp.where(first, low, high) + got.astype(F32)
-
-    qkv_grad, out_grad, small, rel_grad, in_grad, back_grad = [whole_grad(n) for n in range(6)]
-    tall = jnp.concatenate(
-        [out_grad, jnp.broadcast_to(small[None], (devices,) + small.shape)], axis=1
-    ).astype(BF16)
-    tall = sum_blocks(exchange_tensor([tall[d] for d in range(devices)]))
-    wide = jnp.concatenate([qkv_grad, tall.T], axis=1)
-    rel_wide = jnp.pad(rel_grad, ((0, 0), (0, wide.shape[1] - rel_grad.shape[1])))
-    packed = jnp.concatenate(
-        [wide.reshape(groups, -1, wide.shape[1]), rel_wide.reshape(groups, -1, wide.shape[1])],
-        axis=1,
-    ).astype(BF16)
-    shares = jnp.sum(swap_experts(packed).astype(F32), axis=0)
-    mine = width // groups
-    cols = w_query.shape[2]
+        result = jnp.zeros((2,) + own.shape, own.dtype)
+        result = lax.dynamic_update_index_in_dim(result, own, core, 0)
+        return lax.dynamic_update_index_in_dim(result, got, 1 - core, 0)[None]
+
+    attn_grad = whole_grad(grads[0][0], grads[1][0])
+    attn_grad = sum_blocks(exchange_tensor([attn_grad] * devices))
+    attn_grad = jnp.sum(swap_experts(attn_grad.reshape(groups, -1)), axis=0)
+    in_grad, back_grad = grads[0][1]
     return (
         whole_rows(acts),
         whole_rows(row_grads),
-        shares[:mine, 4 * cols][None],
-        shares[:mine, 4 * cols + 1][None],
-        shares[:mine, :cols][None],
-        shares[:mine, cols : 2 * cols][None],
-        shares[:mine, 2 * cols : 3 * cols][None],
-        shares[:mine, 3 * cols : 4 * cols].T[None],
-        shares[mine:, : rel_bias.shape[2]][None],
-        shares[:mine, 4 * cols + 2 :][None],
+        attn_grad[None],
+        *grads[0][2],
         in_grad[None],
         back_grad[None],
     )

time: 792 us -> 653 us (0.82)
  waiting for transfers between devices: 349 us -> 152 us
  starting transfers between devices: 99.7 us -> 212 us
  blocking collectives: 55.5 us -> 0 us
  matrix products: 147 us -> 102 us
  Pallas kernels: 27.2 us -> 52.8 us
  local copies, waits for them, and re-layouts: 33.8 us -> 57.3 us
    ppermute x60 -> x90, waiting for transfers between devices: 286 us -> 127 us  [swap_tensor(): lax.ppermute(block, 'tensor', [(i, i ^ distance) for i in range(devices)])]
    ppermute x0 -> x51, starting transfers between devices: none -> 88.1 us  [shift_experts(): lax.ppermute(block, 'expert', [(i, (i + distance) % groups) for i in rang...]
    all_to_all x6 -> x2, waiting for transfers between devices: 60.5 us -> 4.33 us  [swap_experts(): lax.all_to_all(block, 'expert', split_axis=0, concat_axis=0, tiled=True)]
    all_to_all x3 -> x0, blocking collectives: 55.5 us -> none  [swap_experts(): lax.all_to_all(block, 'expert', split_axis=0, concat_axis=0, tiled=True)]
    ppermute x60 -> x90, starting transfers between devices: 70.7 us -> 112 us  [swap_tensor(): lax.ppermute(block, 'tensor', [(i, i ^ distance) for i in range(devices)])]
    dot_general x12 -> x16, matrix products: 76.1 us -> 37.7 us  [per_expert(): lax.dot_general(left, right, ((contract[:1], contract[1:]), ((0,), (0,)))...]
    pallas_call x0 -> x4, Pallas kernels: none -> 25.8 us  [expert_grads(): pl.pallas_call(functools.partial(grads_kernel, chunks=chunks, per_chunk=p...]
    broadcast_in_dim x4 -> x0, other arithmetic: 17.6 us -> none  [the longest x1 8.92 us: body(): back_grad[None]]
  transfers between devices with their start and end apart: 83 -> 161, of which waited for: 54 -> 58; matrix products, arithmetic and copies ran while one was open for 20% -> 21% of each run, Pallas kernels for 2% -> 6%
where the time goes in v2:
time: 653 us; the launch traced here: 642 us
  starting transfers between devices  212 us (32%)
  waiting for transfers between devices  152 us (23%)
  matrix products  102 us (16%)
  local copies, waits for them, and re-layouts  57.3 us (9%)
  Pallas kernels  52.8 us (8%)
  other arithmetic  46.7 us (7%)
  between operations  18.4 us (3%)
    ppermute x90, waiting for transfers between devices, swap_tensor(): lax.ppermute(block, 'tensor', [(i, i ^ distance) for i in range(devices)])  127 us
    ppermute x90, starting transfers between devices, swap_tensor(): lax.ppermute(block, 'tensor', [(i, i ^ distance) for i in range(devices)])  112 us
    ppermute x51, starting transfers between devices, shift_experts(): lax.ppermute(block, 'expert', [(i, (i + distance) % groups) for i in rang...  88.1 us
    dot_general x16, matrix products, per_expert(): lax.dot_general(left, right, ((contract[:1], contract[1:]), ((0,), (0,)))...  37.7 us
    dot_general x26, matrix products, dot_left(): lax.dot_general(left, right, (((0,), (0,)), ((), ())), preferred_element_...  31.2 us
    unnamed x539, local copies, waits for them, and re-layouts  28 us
    pallas_call x4, Pallas kernels, expert_grads(): pl.pallas_call(functools.partial(grads_kernel, chunks=chunks, per_chunk=p...  25.8 us
    dot_general x28, matrix products, dot(): return jnp.dot(left, right, preferred_element_type=F32)  18.8 us
  transfers between devices with their start and end apart: 161, of which 58 were waited for; matrix products, arithmetic and copies ran while one was open for 21% of the time, Pallas kernels for 6%

profile of v2, /device:TPU:0, one launch (start us, length us, event | category | flops | bytes accessed | tf_op | source)
XLA Modules:
  0.0 641.5 jit_solution(11866400290131733910)
XLA Ops:
  49.9 5.0 shard_map.265
  88.1 6.0 collective-permute-done.29
  99.1 11.4 %collective-permute-done.17 = bf16[2,96,768]{2,1,0:T(8,128)(2,1)S(1)} collective-permute-done((bf16[2,96,768]{2,1,0:T(8,128)(2,1)S(1)}, bf16[2,96,768]{2,1,0:T(8,128)(2,1)S(1)}, u32[]{:S(2)}, u32[]{:S(2)}) %collective-permute-start.17) | collective-permute-done | bytes 294944 | tf_op jit(solution)/shard_map/ppermute | solution.py:235
  159.7 4.6 collective-permute-done.47
  183.2 5.0 shard_map.266
  328.4 8.6 %shard_map.267 = (bf16[1024,576]{1,0:T(8,128)(2,1)S(1)}, f32[3,32,128]{2,1,0:T(8,128)S(1)}) custom-call(f32[32,3]{1,0:T(8,128)S(1)} %copy-done.46, bf16[1024,576]{1,0:T(8,128)(2,1)S(1)} %copy-done.5, f32[2,3,512]{2,1,0:T(4,128)S(1)} %copy-done.52, bf16[1024,192]{1,0:T(8,128)(2,1)S(1)} %copy-done.41), custom_call_target="tpu_custom_call" | custom-call | tf_op jit(solution)/shard_map/pallas_call | solution.py:206
  338.8 5.8 convolution_convert_fusion.1
  351.0 5.8 collective-permute-done.104
  356.9 5.0 collective-permute-done.105
  371.3 4.7 collective-permute-done.108
  406.0 4.9 collective-permute-done.126
  426.2 4.6 shard_map.269
  454.5 5.1 shard_map.271
  476.9 8.4 %shard_map.268 = (bf16[1024,576]{1,0:T(8,128)(2,1)S(1)}, f32[3,32,128]{2,1,0:T(8,128)S(1)}) custom-call(f32[32,3]{1,0:T(8,128)S(1)} %get-tuple-element.333.rel_ref, bf16[1024,576]{1,0:T(8,128)(2,1)S(1)} %copy-done.3, f32[2,3,512]{2,1,0:T(4,128)S(1)} %copy-done.50, bf16[1024,192]{1,0:T(8,128)(2,1)S(1)} %copy-done.42), custom_call_target="tpu_custom_call" | custom-call | tf_op jit(solution)/shard_map/pallas_call | solution.py:206
  504.9 4.6 all-to-all-start
  513.7 9.0 %collective-permute-done.87 = bf16[256,768]{1,0:T(8,128)(2,1)S(1)} collective-permute-done((bf16[256,768]{1,0:T(8,128)(2,1)}, bf16[256,768]{1,0:T(8,128)(2,1)S(1)}, u32[]{:S(2)}, u32[]{:S(2)}) %collective-permute-start.87) | collective-permute-done | bytes 393248 | tf_op jit(solution)/shard_map/ppermute | solution.py:235
  522.7 7.8 %collective-permute-done.86 = bf16[256,768]{1,0:T(8,128)(2,1)S(1)} collective-permute-done((bf16[256,768]{1,0:T(8,128)(2,1)}, bf16[256,768]{1,0:T(8,128)(2,1)S(1)}, u32[]{:S(2)}, u32[]{:S(2)}) %collective-permute-start.86) | collective-permute-done | bytes 393248 | tf_op jit(solution)/shard_map/ppermute | solution.py:235
  530.5 5.2 broadcast_select_fusion.1
  535.8 5.5 convolution_convert_fusion
  557.1 8.1 %shard_map.270 = f32[4,768,768]{2,1,0:T(8,128)} custom-call(s32[1]{0:T(128)} %bitcast.122.pick_ref, bf16[2,384,768]{2,1,0:T(8,128)(2,1)S(1)} %copy-done.13, bf16[2,384,768]{2,1,0:T(8,128)(2,1)S(1)} %copy-done.18, bf16[2,384,768]{2,1,0:T(8,128)(2,1)S(1)} %copy-done.8, bf16[2,384,768]{2,1,0:T(8,128)(2,1)S(1)} %constant_dynamic-update-slice_fusion.21.refs_3_, ...), custom_call_target="tpu_custom_call" | custom-call | flops 1811939328 | bytes 18874368 | tf_op jit(solution)/shard_map/pallas_call | solution.py:377
  565.3 8.1 %shard_map.272 = f32[4,768,768]{2,1,0:T(8,128)} custom-call(s32[1]{0:T(128)} %bitcast.122.pick_ref, bf16[2,384,768]{2,1,0:T(8,128)(2,1)S(1)} %copy-done.24, bf16[2,384,768]{2,1,0:T(8,128)(2,1)S(1)} %copy-done.21, bf16[2,384,768]{2,1,0:T(8,128)(2,1)S(1)} %copy-done.27, bf16[2,384,768]{2,1,0:T(8,128)(2,1)S(1)} %copy-done.30, ...), custom_call_target="tpu_custom_call" | custom-call | flops 1811939328 | bytes 18874368 | tf_op jit(solution)/shard_map/pallas_call | solution.py:377
  588.9 7.0 %collective-permute-done.148 = bf16[256,768]{1,0:T(8,128)(2,1)S(1)} collective-permute-done((bf16[256,768]{1,0:T(8,128)(2,1)S(1)}, bf16[256,768]{1,0:T(8,128)(2,1)S(1)}, u32[]{:S(2)}, u32[]{:S(2)}) %collective-permute-start.148) | collective-permute-done | bytes 393248 | tf_op jit(solution)/shard_map/ppermute | solution.py:235
  597.1 5.2 broadcast_select_fusion
  613.3 4.8 all-to-all-start.1
  (1095 shorter events, 473.0 us)
Async XLA Ops:
  7.2 103.3 %all-gather.3.cloned.1.call-start = ((), (), s32[]{:S(2)}) async-start(), calls=%async_computation.2 | async-start | bytes 14155776 | tf_op jit(solution)/shard_map/all_gather | solution.py:553
  8.0 107.2 %all-gather.5.cloned.1.call-start = ((), (), s32[]{:S(2)}) async-start(), calls=%async_computation.3 | async-start | bytes 14155776 | tf_op jit(solution)/shard_map/all_gather | solution.py:554
  8.3 24.1 %collective-permute-start.6 = (bf16[192,768]{1,0:T(8,128)(2,1)S(1)}, bf16[192,768]{1,0:T(8,128)(2,1)}, u32[]{:S(2)}, u32[]{:S(2)}) collective-permute-start(bf16[192,768]{1,0:T(8,128)(2,1)S(1)} %bitcast.362), channel_id=1, source_target_pairs={{0,3},{1,2},{2,1},{3,0},{4,7},{5,6},{6,5},{7,4},{8,11},{9,10},{10,... | collective-permute-start | bytes 884744 | tf_op jit(solution)/shard_map/ppermute | solution.py:235
  12.2 21.5 %collective-permute-start.5 = (bf16[192,768]{1,0:T(8,128)(2,1)S(1)}, bf16[192,768]{1,0:T(8,128)(2,1)}, u32[]{:S(2)}, u32[]{:S(2)}) collective-permute-start(bf16[192,768]{1,0:T(8,128)(2,1)S(1)} %bitcast.363), channel_id=1, source_target_pairs={{0,2},{1,3},{2,0},{3,1},{4,6},{5,7},{6,4},{7,5},{8,10},{9,11},{10,... | collective-permute-start | bytes 884744 | tf_op jit(solution)/shard_map/ppermute | solution.py:235
  12.7 22.6 %collective-permute-start.4 = (bf16[192,768]{1,0:T(8,128)(2,1)S(1)}, bf16[192,768]{1,0:T(8,128)(2,1)}, u32[]{:S(2)}, u32[]{:S(2)}) collective-permute-start(bf16[192,768]{1,0:T(8,128)(2,1)S(1)} %bitcast.364), channel_id=1, source_target_pairs={{0,1},{1,0},{2,3},{3,2},{4,5},{5,4},{6,7},{7,6},{8,9},{9,8},{10,11... | collective-permute-start | bytes 884744 | tf_op jit(solution)/shard_map/ppermute | solution.py:235
  20.9 27.5 %collective-permute-start.3 = (bf16[768,576]{0,1:T(8,128)(2,1)}, bf16[768,576]{0,1:T(8,128)(2,1)S(1)}, u32[]{:S(2)}, u32[]{:S(2)}) collective-permute-start(bf16[768,576]{0,1:T(8,128)(2,1)} %pad_maximum_fusion.7), channel_id=1, source_target_pairs={{0,16},{16,0},{1,17},{17,1},{2,18},{18,2},{3,19},{19,3},{4,20},{20... | collective-permute-start | bytes 2654216 | tf_op jit(solution)/shard_map/ppermute | solution.py:247
  36.7 22.9 %collective-permute-start.7 = (bf16[4,192,768]{2,1,0:T(8,128)(2,1)S(1)}, bf16[4,192,768]{2,1,0:T(8,128)(2,1)S(1)}, u32[]{:S(2)}, u32[]{:S(2)}) collective-permute-start(bf16[4,192,768]{2,1,0:T(8,128)(2,1)S(1)} %pad_maximum_fusion.4), channel_id=1, source_target_pairs={{0,16},{16,0},{1,17},{17,1},{2,18},{18,2},{3,19},{19,3},{4,20},{20... | collective-permute-start | bytes 3538952 | tf_op jit(solution)/shard_map/ppermute | solution.py:247
  43.4 27.9 %collective-permute-start.12 = (bf16[768,16]{0,1:T(8,128)(2,1)S(1)}, bf16[768,16]{0,1:T(8,128)(2,1)S(1)}, u32[]{:S(2)}, u32[]{:S(2)}) collective-permute-start(bf16[768,16]{0,1:T(8,128)(2,1)S(1)} %bitcast.377), channel_id=1, source_target_pairs={{0,16},{16,0},{1,17},{17,1},{2,18},{18,2},{3,19},{19,3},{4,20},{20... | collective-permute-start | bytes 73736 | tf_op jit(solution)/shard_map/ppermute | solution.py:247
  82.2 28.3 %collective-permute-start.17 = (bf16[2,96,768]{2,1,0:T(8,128)(2,1)S(1)}, bf16[2,96,768]{2,1,0:T(8,128)(2,1)S(1)}, u32[]{:S(2)}, u32[]{:S(2)}) collective-permute-start(bf16[2,96,768]{2,1,0:T(8,128)(2,1)S(1)} %pad_maximum_fusion.9), channel_id=1, source_target_pairs={{0,2},{1,3},{2,0},{3,1},{4,6},{5,7},{6,4},{7,5},{8,10},{9,11},{10,... | collective-permute-start | bytes 884744 | tf_op jit(solution)/shard_map/ppermute | solution.py:235
  86.4 24.1 %collective-permute-start.18 = (bf16[2,96,768]{2,1,0:T(8,128)(2,1)S(1)}, bf16[2,96,768]{2,1,0:T(8,128)(2,1)S(1)}, u32[]{:S(2)}, u32[]{:S(2)}) collective-permute-start(bf16[2,96,768]{2,1,0:T(8,128)(2,1)S(1)} %pad_maximum_fusion.9), channel_id=1, source_target_pairs={{0,3},{1,2},{2,1},{3,0},{4,7},{5,6},{6,5},{7,4},{8,11},{9,10},{10,... | collective-permute-start | bytes 884744 | tf_op jit(solution)/shard_map/ppermute | solution.py:235
  94.2 53.2 %collective-permute-start.48 = (bf16[2,96,768]{2,1,0:T(8,128)(2,1)}, bf16[2,96,768]{2,1,0:T(8,128)(2,1)}, u32[]{:S(2)}, u32[]{:S(2)}) collective-permute-start(bf16[2,96,768]{2,1,0:T(8,128)(2,1)} %pad_maximum_fusion.11), channel_id=1, source_target_pairs={{0,3},{1,2},{2,1},{3,0},{4,7},{5,6},{6,5},{7,4},{8,11},{9,10},{10,... | collective-permute-start | bytes 884744 | tf_op jit(solution)/shard_map/ppermute | solution.py:235
  201.1 19.5 %collective-permute-start.73 = (bf16[2,24,768]{2,1,0:T(8,128)(2,1)S(1)}, bf16[2,24,768]{2,1,0:T(8,128)(2,1)S(1)}, u32[]{:S(2)}, u32[]{:S(2)}) collective-permute-start(bf16[2,24,768]{2,1,0:T(8,128)(2,1)S(1)} %bitcast.405), channel_id=1, source_target_pairs={{0,4},{4,8},{8,12},{12,0},{1,5},{5,9},{9,13},{13,1},{2,6},{6,10},{... | collective-permute-start | bytes 221192 | tf_op jit(solution)/shard_map/ppermute | solution.py:307
  202.0 22.1 %collective-permute-start.74 = (bf16[2,24,768]{2,1,0:T(8,128)(2,1)S(1)}, bf16[2,24,768]{2,1,0:T(8,128)(2,1)S(1)}, u32[]{:S(2)}, u32[]{:S(2)}) collective-permute-start(bf16[2,24,768]{2,1,0:T(8,128)(2,1)S(1)} %bitcast.401), channel_id=1, source_target_pairs={{0,8},{4,12},{8,0},{12,4},{1,9},{5,13},{9,1},{13,5},{2,10},{6,14},... | collective-permute-start | bytes 221192 | tf_op jit(solution)/shard_map/ppermute | solution.py:307
  224.1 22.7 %collective-permute-start.76 = (bf16[2,96,768]{2,1,0:T(8,128)(2,1)S(1)}, bf16[2,96,768]{2,1,0:T(8,128)(2,1)S(1)}, u32[]{:S(2)}, u32[]{:S(2)}) collective-permute-start(bf16[2,96,768]{2,1,0:T(8,128)(2,1)S(1)} %pad_maximum_fusion.14), channel_id=1, source_target_pairs={{0,1},{1,0},{2,3},{3,2},{4,5},{5,4},{6,7},{7,6},{8,9},{9,8},{10,11... | collective-permute-start | bytes 884744 | tf_op jit(solution)/shard_map/ppermute | solution.py:235
  224.7 22.2 %collective-permute-start.77 = (bf16[2,96,768]{2,1,0:T(8,128)(2,1)S(1)}, bf16[2,96,768]{2,1,0:T(8,128)(2,1)S(1)}, u32[]{:S(2)}, u32[]{:S(2)}) collective-permute-start(bf16[2,96,768]{2,1,0:T(8,128)(2,1)S(1)} %pad_maximum_fusion.14), channel_id=1, source_target_pairs={{0,2},{1,3},{2,0},{3,1},{4,6},{5,7},{6,4},{7,5},{8,10},{9,11},{10,... | collective-permute-start | bytes 884744 | tf_op jit(solution)/shard_map/ppermute | solution.py:235
  465.8 19.6 %collective-permute-start.141 = (bf16[209,768]{1,0:T(8,128)(2,1)}, bf16[209,768]{1,0:T(8,128)(2,1)}, u32[]{:S(2)}, u32[]{:S(2)}) collective-permute-start(bf16[209,768]{1,0:T(8,128)(2,1)} %get-tuple-element.231), channel_id=1, source_target_pairs={{0,3},{1,2},{2,1},{3,0},{4,7},{5,6},{6,5},{7,4},{8,11},{9,10},{10,... | collective-permute-start | bytes 963080 | tf_op jit(solution)/shard_map/ppermute | solution.py:235
  469.6 79.5 %collective-permute-start.145 = (bf16[4,768,768]{2,1,0:T(8,128)(2,1)}, bf16[4,768,768]{2,1,0:T(8,128)(2,1)}, u32[]{:S(2)}, u32[]{:S(2)}) collective-permute-start(bf16[4,768,768]{2,1,0:T(8,128)(2,1)} %shard_map.269), channel_id=1, source_target_pairs={{0,16},{16,0},{1,17},{17,1},{2,18},{18,2},{3,19},{19,3},{4,20},{20... | collective-permute-start | bytes 14155784 | tf_op jit(solution)/shard_map/ppermute | solution.py:247
  469.7 95.6 %collective-permute-start.146 = (bf16[4,768,768]{2,1,0:T(8,128)(2,1)}, bf16[4,768,768]{2,1,0:T(8,128)(2,1)}, u32[]{:S(2)}, u32[]{:S(2)}) collective-permute-start(bf16[4,768,768]{2,1,0:T(8,128)(2,1)} %shard_map.271), channel_id=1, source_target_pairs={{0,16},{16,0},{1,17},{17,1},{2,18},{18,2},{3,19},{19,3},{4,20},{20... | collective-permute-start | bytes 14155784 | tf_op jit(solution)/shard_map/ppermute | solution.py:247
  504.9 42.4 %all-to-all-start = ((bf16[4,200,785]{2,1,0:T(8,128)(2,1)}), bf16[4,200,785]{2,1,0:T(8,128)(2,1)}, u32[]{:S(2)}, u32[]{:S(2)}) async-start(bf16[4,200,785]{2,1,0:T(8,128)(2,1)} %pad_maximum_fusion.2), calls=%async_computation | async-start | bytes 2867200 | tf_op jit(solution)/shard_map/all_to_all | solution.py:251
  543.8 29.6 %collective-permute-start.142 = (bf16[256,768]{1,0:T(8,128)(2,1)}, bf16[256,768]{1,0:T(8,128)(2,1)}, u32[]{:S(2)}, u32[]{:S(2)}) collective-permute-start(bf16[256,768]{1,0:T(8,128)(2,1)} %get-tuple-element.224), channel_id=1, source_target_pairs={{0,1},{1,0},{2,3},{3,2},{4,5},{5,4},{6,7},{7,6},{8,9},{9,8},{10,11... | collective-permute-start | bytes 1179656 | tf_op jit(solution)/shard_map/ppermute | solution.py:235
  544.5 28.9 %collective-permute-start.143 = (bf16[256,768]{1,0:T(8,128)(2,1)}, bf16[256,768]{1,0:T(8,128)(2,1)}, u32[]{:S(2)}, u32[]{:S(2)}) collective-permute-start(bf16[256,768]{1,0:T(8,128)(2,1)} %get-tuple-element.223), channel_id=1, source_target_pairs={{0,2},{1,3},{2,0},{3,1},{4,6},{5,7},{6,4},{7,5},{8,10},{9,11},{10,... | collective-permute-start | bytes 1179656 | tf_op jit(solution)/shard_map/ppermute | solution.py:235
  545.9 27.5 %collective-permute-start.144 = (bf16[256,768]{1,0:T(8,128)(2,1)}, bf16[256,768]{1,0:T(8,128)(2,1)}, u32[]{:S(2)}, u32[]{:S(2)}) collective-permute-start(bf16[256,768]{1,0:T(8,128)(2,1)} %get-tuple-element.222), channel_id=1, source_target_pairs={{0,3},{1,2},{2,1},{3,0},{4,7},{5,6},{6,5},{7,4},{8,11},{9,10},{10,... | collective-permute-start | bytes 1179656 | tf_op jit(solution)/shard_map/ppermute | solution.py:235
  549.1 60.2 %collective-permute-start.88 = (bf16[1024,768]{0,1:T(8,128)(2,1)}, bf16[1024,768]{0,1:T(8,128)(2,1)}, u32[]{:S(2)}, u32[]{:S(2)}) collective-permute-start(bf16[1024,768]{0,1:T(8,128)(2,1)} %get-tuple-element.218), channel_id=1, source_target_pairs={{0,16},{16,0},{1,17},{17,1},{2,18},{18,2},{3,19},{19,3},{4,20},{20... | collective-permute-start | bytes 4718600 | tf_op jit(solution)/shard_map/ppermute | solution.py:247
  602.3 26.8 %collective-permute-start.152 = (bf16[1024,768]{0,1:T(8,128)(2,1)}, bf16[1024,768]{0,1:T(8,128)(2,1)}, u32[]{:S(2)}, u32[]{:S(2)}) collective-permute-start(bf16[1024,768]{0,1:T(8,128)(2,1)} %get-tuple-element.216), channel_id=1, source_target_pairs={{0,16},{16,0},{1,17},{17,1},{2,18},{18,2},{3,19},{19,3},{4,20},{20... | collective-permute-start | bytes 4718600 | tf_op jit(solution)/shard_map/ppermute | solution.py:247
  (386 other events, 3322.8 us)
Sparse Core Ops, SparseCore 0:
  9.6 24.5 all-gather.2
  35.8 22.9 all-gather.4

commit v3 on v2

--- a/solution.py
+++ b/solution.py
@@ -259,7 +259,7 @@
 
 
 def chunks_of(local):
-    return 2 if local % 2 == 0 else 1
+    return 1
 
 
 def make_plan(route_rows, keep_rows, experts, capacity):
@@ -313,10 +313,6 @@
     return jnp.concatenate([shift_experts(rows[d], d) for d in range(groups)], axis=1)
 
 
-def all_shares(got):
-    return jnp.concatenate(gather_tensor(got), axis=1)
-
-
 def send_tokens(rows, places, local):
     per_chunk = local // len(places)
     return [to_groups(dot(place, rows).astype(BF16), per_chunk) for place in places]
@@ -324,11 +320,8 @@
 
 def from_experts(parts, place):
     groups = lax.axis_size("expert")
-    devices = lax.axis_size("tensor")
-    local, slots, width = parts.shape
-    own = slots // devices
-    parts = parts.astype(BF16)
-    blocks = exchange_tensor([parts[:, d * own : (d + 1) * own] for d in range(devices)])
+    local, own, width = parts[0].shape
+    blocks = exchange_tensor(parts)
     summed = sum_blocks(blocks).astype(BF16)
     share = own // groups
     back = [
@@ -338,10 +331,79 @@
     return dot_left(place, jnp.concatenate(back, axis=0))
 
 
-def per_expert(left, right, contract):
-    return lax.dot_general(
-        left, right, ((contract[:1], contract[1:]), ((0,), (0,))), preferred_element_type=F32
-    )
+def ffn_kernel(*refs, devices):
+    blocks, first_ref, second_ref = refs[:devices], refs[devices], refs[devices + 1]
+    rows_ref, hidden_ref, slope_ref = refs[devices + 2 : devices + 5]
+    parts = refs[devices + 5 :]
+    size = blocks[0].shape[1]
+    for d in range(devices):
+        rows_ref[0, d * size : (d + 1) * size, :] = blocks[d][0]
+    inner = dot(rows_ref[0], first_ref[0, 0])
+    cumulative = 0.5 * (1.0 + lax.erf(inner * np.float32(np.sqrt(0.5))))
+    density = jnp.exp(-0.5 * inner * inner) * np.float32(1.0 / np.sqrt(2.0 * np.pi))
+    hidden = (inner * cumulative).astype(BF16)
+    hidden_ref[0] = hidden
+    slope_ref[0] = (cumulative + inner * density).astype(BF16)
+    out = dot(hidden, second_ref[0, 0]).astype(BF16)
+    for d in range(devices):
+        parts[d][0] = out[d * size : (d + 1) * size]
+
+
+def ffn_back_kernel(*refs, devices, gated):
+    blocks, refs = refs[:devices], refs[devices:]
+    if gated:
+        factor_ref, refs = refs[0], refs[1:]
+    first_ref, second_ref, slope_ref, grad_ref, inner_ref = refs[:5]
+    parts = refs[5:]
+    size = blocks[0].shape[1]
+    for d in range(devices):
+        block = blocks[d][0]
+        if gated:
+            factor = factor_ref[0, d * size : (d + 1) * size, :]
+            block = (factor * block.astype(F32)).astype(BF16)
+        grad_ref[0, d * size : (d + 1) * size, :] = block
+    hidden_grad = dot_right(grad_ref[0], second_ref[0, 0])
+    inner_grad = (hidden_grad * slope_ref[0].astype(F32)).astype(BF16)
+    inner_ref[0] = inner_grad
+    out = dot_right(inner_grad, first_ref[0, 0]).astype(BF16)
+    for d in range(devices):
+        parts[d][0] = out[d * size : (d + 1) * size]
+
+
+def ffn_call(kernel, blocks, weights, others, widths):
+    first, second, layer, start = weights
+    devices = len(blocks)
+    count, size, width = blocks[0].shape
+    slots = devices * size
+    inner = first.shape[3]
+
+    def rows(height, cols):
+        return pl.BlockSpec((1, height, cols), lambda e: (e, 0, 0))
+
+    def weight(array):
+        return pl.BlockSpec((1, 1) + array.shape[2:], lambda e: (layer, start + e, 0, 0))
+
+    before = [other for other in others if other.shape[2] == 1]
+    after = [other for other in others if other.shape[2] != 1]
+    return pl.pallas_call(
+        kernel,
+        grid=(count,),
+        in_specs=[rows(size, width)] * devices
+        + [rows(slots, 1) for _ in before]
+        + [weight(first), weight(second)]
+        + [rows(slots, other.shape[2]) for other in after],
+        out_specs=[rows(slots, cols) for cols in widths] + [rows(size, width)] * devices,
+        out_shape=[jax.ShapeDtypeStruct((count, slots, cols), BF16) for cols in widths]
+        + [jax.ShapeDtypeStruct((count, size, width), BF16)] * devices,
+        compiler_params=pltpu.CompilerParams(
+            dimension_semantics=("arbitrary",), vmem_limit_bytes=40 << 20
+        ),
+        cost_estimate=pl.CostEstimate(
+            flops=4 * count * slots * width * inner,
+            transcendentals=2 * count * slots * inner,
+            bytes_accessed=4 * count * (width * inner + 2 * slots * width),
+        ),
+    )(*blocks, *before, first, second, *after)
 
 
 def grads_kernel(pick_ref, *refs, chunks, per_chunk):
@@ -397,10 +459,10 @@
 
 
 def layer_forward(rows_in, weights, rel, plan, ahead, with_gates):
-    attn_gain, ffn_gain, w_qkv, w_out, w_router, w_in, w_back = weights
+    attn_gain, ffn_gain, w_qkv, w_out, w_router, w_in, w_back, layer = weights
     deal, deal_own, places, chosen, kept = plan
     devices = lax.axis_size("tensor")
-    local = sum(block.shape[0] for block in w_in)
+    local, width, inner_width = w_in.shape[1:]
     layer_in = rows_in.astype(F32)
     scale_one = root_mean(layer_in)
     normed = (layer_in * scale_one * attn_gain).astype(BF16)
@@ -419,17 +481,22 @@
     probs = jax.nn.softmax(dot(normed_two, w_router), axis=-1)
     gate = jnp.sum(probs * chosen, axis=-1)
     gates = send_gates(kept * gate, places, local) if with_gates else None
-    incoming = [all_shares(got) for got in send_tokens(normed_two, places, local)]
+    sent = [gather_tensor(got) for got in send_tokens(normed_two, places, local)]
     if not with_gates:
-        incoming[-1], ahead = lax.optimization_barrier((incoming[-1], ahead))
-    hidden, slope, per_token = [], [], 0.0
-    for place, rows, first, second in zip(places, incoming, w_in, w_back):
-        inner = per_expert(rows, first, (2, 1))
-        cumulative = 0.5 * (1.0 + lax.erf(inner * np.float32(np.sqrt(0.5))))
-        density = jnp.exp(-0.5 * inner * inner) * np.float32(1.0 / np.sqrt(2.0 * np.pi))
-        hidden.append((inner * cumulative).astype(BF16))
-        slope.append((cumulative + inner * density).astype(BF16))
-        parts = per_expert(hidden[-1], second, (2, 1)).astype(BF16)
+        sent[-1], ahead = lax.optimization_barrier((sent[-1], ahead))
+    incoming, hidden, slope, per_token = [], [], [], 0.0
+    for n, place in enumerate(places):
+        chosen_weights = (w_in, w_back, layer, n * local // len(places))
+        rows, low, steep, *parts = ffn_call(
+            functools.partial(ffn_kernel, devices=devices),
+            sent[n],
+            chosen_weights,
+            [],
+            (width, inner_width, inner_width),
+        )
+        incoming.append(rows)
+        hidden.append(low)
+        slope.append(steep)
         if with_gates:
             parts, gates = lax.optimization_barrier((parts, gates))
         per_token = per_token + from_experts(parts, place)
@@ -457,31 +524,35 @@
     ]
     factors = jnp.concatenate(factors, axis=1)
     got = jnp.concatenate([shift_experts(factors[d], d) for d in range(groups)], axis=1)
-    return jnp.split(all_shares(got)[:, :, None], len(places))
+    got = jnp.concatenate(gather_tensor(got), axis=1)
+    return jnp.split(got[:, :, None], len(places))
 
 
 def layer_backward(saved, rows_grad, weights, rel, plan, early, gates, finish):
-    attn_gain, ffn_gain, w_qkv, w_out, w_router, w_in, w_back = weights
+    attn_gain, ffn_gain, w_qkv, w_out, w_router, w_in, w_back, layer = weights
     deal, deal_own, places, chosen, kept = plan
     own_in, normed, qkv, lse, heads, middle, normed_two, probs, gate = saved[:9]
     incoming, hidden, slope, per_token = saved[9:]
     devices = lax.axis_size("tensor")
-    local = sum(block.shape[0] for block in w_in)
+    local, width, inner_width = w_in.shape[1:]
     grad_out = dot(deal_own, rows_grad)
     gated = ((kept * gate)[:, None] * grad_out).astype(BF16)
     gate_grad = kept * jnp.sum(grad_out * per_token, axis=-1)
     if early is None:
-        expert_grad = [all_shares(got) for got in send_tokens(gated, places, local)]
-    else:
-        expert_grad = [
-            (factor * rows.astype(F32)).astype(BF16) for factor, rows in zip(gates, early)
-        ]
-    input_rows, inner_grads = 0.0, []
+        early = [gather_tensor(got) for got in send_tokens(gated, places, local)]
+        gates = None
+    input_rows, inner_grads, expert_grad = 0.0, [], []
     for n, place in enumerate(places):
-        hidden_grad = per_expert(expert_grad[n], w_back[n], (2, 2))
-        inner_grad = (hidden_grad * slope[n].astype(F32)).astype(BF16)
-        input_rows = input_rows + from_experts(per_expert(inner_grad, w_in[n], (2, 2)), place)
-        inner_grads.append(inner_grad)
+        rows, low, *parts = ffn_call(
+            functools.partial(ffn_back_kernel, devices=devices, gated=gates is not None),
+            early[n],
+            (w_in, w_back, layer, n * local // len(places)),
+            ([] if gates is None else [gates[n]]) + [slope[n]],
+            (width, inner_width),
+        )
+        expert_grad.append(rows)
+        inner_grads.append(low)
+        input_rows = input_rows + from_experts(parts, place)
     logit_grad = (probs * (chosen - gate[:, None]) * gate_grad[:, None]).astype(BF16)
     router_grad = dot_left(normed_two, logit_grad)
     normed_two_grad = input_rows + dot_right(logit_grad, w_router)
@@ -506,10 +577,10 @@
     normed_grad = sum_blocks(blocks)
     layer_part, attn_grad = norm_back(normed_grad, own_in, attn_gain)
     layer_grad = (middle_grad + layer_part).astype(BF16)
-    last = finish[1](qkv_grad, rel_grad, beside)
+    last, loose = finish[1](qkv_grad, rel_grad, attn_grad, beside)
     blocks, last = lax.optimization_barrier((gather_tensor(layer_grad), last))
     rows_out = dot_left(deal, jnp.concatenate(blocks, axis=0)).astype(BF16)
-    return (rows_out, (attn_grad, fill, last))
+    return (rows_out, (fill, loose, last))
 
 
 def body(
@@ -557,7 +628,6 @@
     got_ints = swap_section(sent_ints)
     ints_pair = (jnp.where(first, own_ints, got_ints), jnp.where(first, got_ints, own_ints))
 
-    chunks = chunks_of(w_in.shape[1])
     weights, rels, plans = [], [], []
     for s in range(2):
         weights.append(
@@ -567,8 +637,9 @@
                 qkv_pair[s],
                 out_pair[s],
                 router_pair[s],
-                jnp.split(in_all[s], chunks),
-                jnp.split(back_all[s], chunks),
+                in_all,
+                back_all,
+                s,
             )
         )
         rels.append(rel_pair[s].astype(F32))
@@ -582,7 +653,7 @@
     for s in range(2):
         rows, kept, ahead, gates = layer_forward(rows, weights[s], rels[s], plans[s], ahead, s == 1)
         if s == 0:
-            ahead = [all_shares(got) for got in ahead]
+            ahead = [gather_tensor(got) for got in ahead]
         acts.append(rows)
         saved.append(kept)
     def whole_grad(low, high):
@@ -592,6 +663,13 @@
     own_layer = core.reshape(1)
     mine = width // groups
     cols = w_query.shape[2]
+    def whole_rows(pair):
+        own = jnp.where(first, pair[0], pair[1])
+        got = swap_section(jnp.where(first, pair[1], pair[0]))
+        result = jnp.zeros((2,) + own.shape, own.dtype)
+        result = lax.dynamic_update_index_in_dim(result, own, core, 0)
+        return lax.dynamic_update_index_in_dim(result, got, 1 - core, 0)[None]
+
     held_experts, held_attention = [], []
 
     def expert_part(inner_grads, expert_grad, out_grad, small):
@@ -612,11 +690,11 @@
         ).astype(BF16)
         return (sum_blocks(exchange_tensor([tall[d] for d in range(devices)])), (in_grad, back_grad))
 
-    def attention_part(qkv_grad, rel_grad, tall):
+    def attention_part(qkv_grad, rel_grad, attn_grad, tall):
         held = held_attention
-        held.append((qkv_grad, rel_grad))
+        held.append((qkv_grad, rel_grad, attn_grad))
         if len(held) < 2:
-            return ()
+            return ((), ())
         wide = jnp.concatenate([whole_grad(qkv_grad, held[0][0]), tall.T], axis=1)
         rel_sum = whole_grad(rel_grad, held[0][1])
         rel_wide = jnp.pad(rel_sum, ((0, 0), (0, wide.shape[1] - rel_sum.shape[1])))
@@ -625,7 +703,9 @@
             axis=1,
         ).astype(BF16)
         shares = jnp.sum(swap_experts(packed).astype(F32), axis=0)
-        return (
+        attn_sum = sum_blocks(exchange_tensor([whole_grad(attn_grad, held[0][2])] * devices))
+        attn_sum = jnp.sum(swap_experts(attn_sum.reshape(groups, -1)), axis=0)
+        tied = (
             shares[:mine, 4 * cols][None],
             shares[:mine, :cols][None],
             shares[:mine, cols : 2 * cols][None],
@@ -634,6 +714,7 @@
             shares[mine:, : rel_bias.shape[2]][None],
             shares[:mine, 4 * cols + 1 :][None],
         )
+        return (tied, (attn_sum[None],))
 
     grads = [None, None]
     row_grads = [None, None]
@@ -651,21 +732,11 @@
         )
         row_grads[s] = rows
 
-    def whole_rows(pair):
-        own = jnp.where(first, pair[0], pair[1])
-        got = swap_section(jnp.where(first, pair[1], pair[0]))
-        result = jnp.zeros((2,) + own.shape, own.dtype)
-        result = lax.dynamic_update_index_in_dim(result, own, core, 0)
-        return lax.dynamic_update_index_in_dim(result, got, 1 - core, 0)[None]
-
-    attn_grad = whole_grad(grads[0][0], grads[1][0])
-    attn_grad = sum_blocks(exchange_tensor([attn_grad] * devices))
-    attn_grad = jnp.sum(swap_experts(attn_grad.reshape(groups, -1)), axis=0)
-    in_grad, back_grad = grads[0][1]
+    in_grad, back_grad = grads[0][0]
     return (
         whole_rows(acts),
         whole_rows(row_grads),
-        attn_grad[None],
+        *grads[0][1],
         *grads[0][2],
         in_grad[None],
         back_grad[None],

time: 653 us -> 638 us (0.977)
  starting transfers between devices: 212 us -> 148 us
  waiting for transfers between devices: 152 us -> 195 us
  matrix products: 102 us -> 67.8 us
  Pallas kernels: 52.8 us -> 86 us
  local copies, waits for them, and re-layouts: 57.3 us -> 73.7 us
    dot_general x16 -> x0, matrix products: 37.7 us -> none  [per_expert(): lax.dot_general(left, right, ((contract[:1], contract[1:]), ((0,), (0,)))...]
    ppermute x51 -> x27, starting transfers between devices: 88.1 us -> 53.5 us  [shift_experts(): lax.ppermute(block, 'expert', [(i, (i + distance) % groups) for i in rang...]
    pallas_call x0 -> x4, Pallas kernels: none -> 32.7 us  [ffn_call(): pl.pallas_call(kernel, grid=(count,), in_specs=[rows(size, width)] * devi...]
    ppermute x90 -> x66, starting transfers between devices: 112 us -> 81.9 us  [swap_tensor(): lax.ppermute(block, 'tensor', [(i, i ^ distance) for i in range(devices)])]
    ppermute x51 -> x27, waiting for transfers between devices: 16.5 us -> 44.5 us  [shift_experts(): lax.ppermute(block, 'expert', [(i, (i + distance) % groups) for i in rang...]
    ppermute x90 -> x66, waiting for transfers between devices: 127 us -> 142 us  [swap_tensor(): lax.ppermute(block, 'tensor', [(i, i ^ distance) for i in range(devices)])]
    unnamed x539 -> x471, local copies, waits for them, and re-layouts: 28 us -> 41.1 us
    dot_general x26 -> x22, matrix products: 31.2 us -> 35 us  [dot_left(): lax.dot_general(left, right, (((0,), (0,)), ((), ())), preferred_element_...]
  transfers between devices with their start and end apart: 161 -> 113, of which waited for: 58 -> 54; matrix products, arithmetic and copies ran while one was open for 21% -> 18% of each run, Pallas kernels for 6% -> 8%
where the time goes in v3:
time: 638 us; the launch traced here: 628 us
  waiting for transfers between devices  195 us (31%)
  starting transfers between devices  148 us (23%)
  Pallas kernels  86 us (13%)
  local copies, waits for them, and re-layouts  73.7 us (12%)
  matrix products  67.8 us (11%)
  other arithmetic  40.4 us (6%)
  between operations  17.6 us (3%)
    ppermute x66, waiting for transfers between devices, swap_tensor(): lax.ppermute(block, 'tensor', [(i, i ^ distance) for i in range(devices)])  142 us
    ppermute x66, starting transfers between devices, swap_tensor(): lax.ppermute(block, 'tensor', [(i, i ^ distance) for i in range(devices)])  81.9 us
    ppermute x27, starting transfers between devices, shift_experts(): lax.ppermute(block, 'expert', [(i, (i + distance) % groups) for i in rang...  53.5 us
    ppermute x27, waiting for transfers between devices, shift_experts(): lax.ppermute(block, 'expert', [(i, (i + distance) % groups) for i in rang...  44.5 us
    unnamed x471, local copies, waits for them, and re-layouts  41.1 us
    dot_general x22, matrix products, dot_left(): lax.dot_general(left, right, (((0,), (0,)), ((), ())), preferred_element_...  35 us
    pallas_call x4, Pallas kernels, ffn_call(): pl.pallas_call(kernel, grid=(count,), in_specs=[rows(size, width)] * devi...  32.7 us
    pallas_call x4, Pallas kernels, expert_grads(): pl.pallas_call(functools.partial(grads_kernel, chunks=chunks, per_chunk=p...  25.9 us
  transfers between devices with their start and end apart: 113, of which 54 were waited for; matrix products, arithmetic and copies ran while one was open for 18% of the time, Pallas kernels for 8%

profile of v3, /device:TPU:0, one launch (start us, length us, event | category | flops | bytes accessed | tf_op | source)
XLA Modules:
  0.0 627.8 jit_solution(1560405656944840069)
XLA Ops:
  80.6 9.4 %collective-permute-done.17.refs_2_ = bf16[4,96,768]{2,1,0:T(8,128)(2,1)S(1)} collective-permute-done((bf16[4,96,768]{2,1,0:T(8,128)(2,1)S(1)}, bf16[4,96,768]{2,1,0:T(8,128)(2,1)S(1)}, u32[]{:S(2)}, u32[]{:S(2)}) %collective-permute-start.17) | collective-permute-done | bytes 589856 | tf_op jit(solution)/shard_map/ppermute | solution.py:235
  94.8 7.5 %shard_map.248 = (bf16[4,384,768]{2,1,0:T(8,128)(2,1)S(1)}, bf16[4,384,768]{2,1,0:T(8,128)(2,1)S(1)}, bf16[4,384,768]{2,1,0:T(8,128)(2,1)S(1)}, bf16[4,96,768]{2...) custom-call(bf16[4,96,768]{2,1,0:T(8,128)(2,1)S(1)} %pad_maximum_fus, ...), custom_call_target="tpu_custom_call" | custom-call | flops 3623878656 | bytes 18874368 | tf_op jit(solution)/shard_map/pallas_call | solution.py:388
  110.7 9.3 %collective-permute-done.22 = bf16[4,96,768]{2,1,0:T(8,128)(2,1)S(1)} collective-permute-done((bf16[4,96,768]{2,1,0:T(8,128)(2,1)S(1)}, bf16[4,96,768]{2,1,0:T(8,128)(2,1)S(1)}, u32[]{:S(2)}, u32[]{:S(2)}) %collective-permute-start.22) | collective-permute-done | bytes 589856 | tf_op jit(solution)/shard_map/ppermute | solution.py:235
  120.0 10.3 %collective-permute-done.23 = bf16[4,96,768]{2,1,0:T(8,128)(2,1)S(1)} collective-permute-done((bf16[4,96,768]{2,1,0:T(8,128)(2,1)S(1)}, bf16[4,96,768]{2,1,0:T(8,128)(2,1)S(1)}, u32[]{:S(2)}, u32[]{:S(2)}) %collective-permute-start.23) | collective-permute-done | bytes 589856 | tf_op jit(solution)/shard_map/ppermute | solution.py:235
  140.6 5.4 collective-permute-done.26
  154.0 5.9 collective-permute-done.28
  162.0 8.3 %collective-permute-done.29 = bf16[256,768]{1,0:T(8,128)(2,1)S(1)} collective-permute-done((bf16[256,768]{1,0:T(8,128)(2,1)S(1)}, bf16[256,768]{1,0:T(8,128)(2,1)S(1)}, u32[]{:S(2)}, u32[]{:S(2)}) %collective-permute-start.29) | collective-permute-done | bytes 393248 | tf_op jit(solution)/shard_map/ppermute | solution.py:235
  181.0 9.8 %collective-permute-done.32.refs_2_ = bf16[4,96,768]{2,1,0:T(8,128)(2,1)S(1)} collective-permute-done((bf16[4,96,768]{2,1,0:T(8,128)(2,1)S(1)}, bf16[4,96,768]{2,1,0:T(8,128)(2,1)S(1)}, u32[]{:S(2)}, u32[]{:S(2)}) %collective-permute-start.32) | collective-permute-done | bytes 589856 | tf_op jit(solution)/shard_map/ppermute | solution.py:235
  227.3 10.1 %collective-permute-start.45 = (f32[4,24]{1,0:T(4,128)}, f32[4,24]{1,0:T(4,128)}, u32[]{:S(2)}, u32[]{:S(2)}) collective-permute-start(f32[4,24]{1,0:T(4,128)} %squeeze.189), channel_id=1, source_target_pairs={{0,12},{4,0},{8,4},{12,8},{1,13},{5,1},{9,5},{13,9},{2,14},{6,2},{... | collective-permute-start | bytes 1160 | tf_op jit(solution)/shard_map/ppermute | solution.py:307
  250.6 8.7 %shard_map.250 = (bf16[4,384,768]{2,1,0:T(8,128)(2,1)S(1)}, bf16[4,384,768]{2,1,0:T(8,128)(2,1)S(1)}, bf16[4,384,768]{2,1,0:T(8,128)(2,1)S(1)}, bf16[4,96,768]{2...) custom-call(bf16[4,96,768]{2,1,0:T(8,128)(2,1)S(1)} %pad_maximum_fusio, ...), custom_call_target="tpu_custom_call" | custom-call | flops 3623878656 | bytes 18874368 | tf_op jit(solution)/shard_map/pallas_call | solution.py:388
  274.9 7.3 %shard_map.251 = (bf16[4,384,768]{2,1,0:T(8,128)(2,1)S(1)}, bf16[4,384,768]{2,1,0:T(8,128)(2,1)S(1)}, bf16[4,96,768]{2,1,0:T(8,128)(2,1)S(1)}, bf16[4,96,768]{2,...) custom-call(bf16[4,96,768]{2,1,0:T(8,128)(2,1)S(1)} %copy-done.32, ...), custom_call_target="tpu_custom_call" | custom-call | flops 3623878656 | bytes 18874368 | tf_op jit(solution)/shard_map/pallas_call | solution.py:388
  287.1 7.6 %collective-permute-done.51 = bf16[4,96,768]{2,1,0:T(8,128)(2,1)} collective-permute-done((bf16[4,96,768]{2,1,0:T(8,128)(2,1)}, bf16[4,96,768]{2,1,0:T(8,128)(2,1)}, u32[]{:S(2)}, u32[]{:S(2)}) %collective-permute-start.51) | collective-permute-done | bytes 589856 | tf_op jit(solution)/shard_map/ppermute | solution.py:235
  340.9 8.8 %shard_map.252 = (bf16[1024,576]{1,0:T(8,128)(2,1)S(1)}, f32[3,32,128]{2,1,0:T(8,128)S(1)}) custom-call(f32[32,3]{1,0:T(8,128)S(1)} %copy-done.52, bf16[1024,576]{1,0:T(8,128)(2,1)S(1)} %copy-done.26, f32[2,3,512]{2,1,0:T(4,128)S(1)} %copy-done.57, bf16[1024,192]{1,0:T(8,128)(2,1)S(1)} %copy.156.grad_ref), custom_call_target="tpu_custom_call" | custom-call | tf_op jit(solution)/shard_map/pallas_call | solution.py:206
  350.9 5.8 convolution_convert_fusion.1
  367.5 6.3 %collective-permute-done.70 = bf16[256,768]{1,0:T(8,128)(2,1)S(1)} collective-permute-done((bf16[256,768]{1,0:T(8,128)(2,1)S(1)}, bf16[256,768]{1,0:T(8,128)(2,1)S(1)}, u32[]{:S(2)}, u32[]{:S(2)}) %collective-permute-start.70) | collective-permute-done | bytes 393248 | tf_op jit(solution)/shard_map/ppermute | solution.py:235
  384.0 6.2 collective-permute-done.72
  414.7 7.1 %collective-permute-done.78.refs_2_ = bf16[4,96,768]{2,1,0:T(8,128)(2,1)} collective-permute-done((bf16[4,96,768]{2,1,0:T(8,128)(2,1)S(1)}, bf16[4,96,768]{2,1,0:T(8,128)(2,1)}, u32[]{:S(2)}, u32[]{:S(2)}) %collective-permute-start.78) | collective-permute-done | bytes 589856 | tf_op jit(solution)/shard_map/ppermute | solution.py:235
  423.5 9.1 %shard_map.253 = (bf16[4,384,768]{2,1,0:T(8,128)(2,1)S(1)}, bf16[4,384,768]{2,1,0:T(8,128)(2,1)S(1)}, bf16[4,96,768]{2,1,0:T(8,128)(2,1)S(1)}, bf16[4,96,768]{2,...) custom-call(bf16[4,96,768]{2,1,0:T(8,128)(2,1)S(1)} %pad_maximum_fusion.9.refs_0_, ...), custom_call_target="tpu_custom_call" | custom-call | flops 3623878656 | bytes 18874368 | tf_op jit(solution)/shard_map/pallas_call | solution.py:388
  445.7 7.5 %collective-permute-done.81 = bf16[4,96,768]{2,1,0:T(8,128)(2,1)S(1)} collective-permute-done((bf16[4,96,768]{2,1,0:T(8,128)(2,1)}, bf16[4,96,768]{2,1,0:T(8,128)(2,1)S(1)}, u32[]{:S(2)}, u32[]{:S(2)}) %collective-permute-start.81) | collective-permute-done | bytes 589856 | tf_op jit(solution)/shard_map/ppermute | solution.py:235
  487.6 8.6 %shard_map.254 = (bf16[1024,576]{1,0:T(8,128)(2,1)S(1)}, f32[3,32,128]{2,1,0:T(8,128)S(1)}) custom-call(f32[32,3]{1,0:T(8,128)S(1)} %get-tuple-element.333.rel_ref, bf16[1024,576]{1,0:T(8,128)(2,1)S(1)} %copy-done.24, f32[2,3,512]{2,1,0:T(4,128)S(1)} %copy-done.55, bf16[1024,192]{1,0:T(8,128)(2,1)S(1)} %copy.158.grad_ref), custom_call_target="tpu_custom_call" | custom-call | tf_op jit(solution)/shard_map/pallas_call | solution.py:206
  508.3 5.4 convolution_convert_fusion
  539.3 8.8 %shard_map.258 = f32[4,768,768]{2,1,0:T(8,128)} custom-call(s32[1]{0:T(128)} %bitcast.75.pick_ref, bf16[4,384,768]{2,1,0:T(8,128)(2,1)S(1)} %copy-done.4, bf16[4,384,768]{2,1,0:T(8,128)(2,1)S(1)} %copy-done.10, bf16[4,384,768]{2,1,0:T(8,128)(2,1)S(1)} %copy-done.22, bf16[4,384,768]{2,1,0:T(8,128)(2,1)S(1)} %copy-done.16, ...), custom_call_target="tpu_custom_call" | custom-call | flops 1811939328 | bytes 18874368 | tf_op jit(solution)/shard_map/pallas_call | solution.py:439
  548.1 7.8 %shard_map.256 = f32[4,768,768]{2,1,0:T(8,128)} custom-call(s32[1]{0:T(128)} %bitcast.75.pick_ref, bf16[4,384,768]{2,1,0:T(8,128)(2,1)S(1)} %get-tuple-element.138.refs_0_, bf16[4,384,768]{2,1,0:T(8,128)(2,1)S(1)} %copy-done.7, bf16[4,384,768]{2,1,0:T(8,128)(2,1)S(1)} %copy-done.19, bf16[4,384,768]{2,1,0:T(8,128)(2,1)S(1)} %copy-done.13, ...), custom_call_target="tpu_custom_call" | custom-call | flops 1811939328 | bytes 18874368 | tf_op jit(solution)/shard_map/pallas_call | solution.py:439
  566.5 13.2 %collective-permute-done.100 = bf16[256,768]{1,0:T(8,128)(2,1)S(1)} collective-permute-done((bf16[256,768]{1,0:T(8,128)(2,1)}, bf16[256,768]{1,0:T(8,128)(2,1)S(1)}, u32[]{:S(2)}, u32[]{:S(2)}) %collective-permute-start.100) | collective-permute-done | bytes 393248 | tf_op jit(solution)/shard_map/ppermute | solution.py:235
  (875 shorter events, 415.7 us)
Async XLA Ops:
  7.2 84.4 %all-gather.3.cloned.1.call-start = ((), (), s32[]{:S(2)}) async-start(), calls=%async_computation.2 | async-start | bytes 14155776 | tf_op jit(solution)/shard_map/all_gather | solution.py:624
  8.0 83.7 %all-gather.5.cloned.1.call-start = ((), (), s32[]{:S(2)}) async-start(), calls=%async_computation.3 | async-start | bytes 14155776 | tf_op jit(solution)/shard_map/all_gather | solution.py:625
  62.5 27.5 %collective-permute-start.17 = (bf16[4,96,768]{2,1,0:T(8,128)(2,1)S(1)}, bf16[4,96,768]{2,1,0:T(8,128)(2,1)S(1)}, u32[]{:S(2)}, u32[]{:S(2)}) collective-permute-start(bf16[4,96,768]{2,1,0:T(8,128)(2,1)S(1)} %pad_maximum_fusion.6.refs_0_), channel_id=1, source_target_pairs={{0,2},{1,3},{2,0},{3,1},{4,6},{5,7},{6,4},{7,5},{8,10},{9,11},{10,... | collective-permute-start | bytes 1769480 | tf_op jit(solution)/shard_map/ppermute | solution.py:235
  63.1 27.7 %collective-permute-start.18 = (bf16[4,96,768]{2,1,0:T(8,128)(2,1)S(1)}, bf16[4,96,768]{2,1,0:T(8,128)(2,1)S(1)}, u32[]{:S(2)}, u32[]{:S(2)}) collective-permute-start(bf16[4,96,768]{2,1,0:T(8,128)(2,1)S(1)} %pad_maximum_fusion.6.refs_0_), channel_id=1, source_target_pairs={{0,3},{1,2},{2,1},{3,0},{4,7},{5,6},{6,5},{7,4},{8,11},{9,10},{10,... | collective-permute-start | bytes 1769480 | tf_op jit(solution)/shard_map/ppermute | solution.py:235
  104.1 26.3 %collective-permute-start.23 = (bf16[4,96,768]{2,1,0:T(8,128)(2,1)S(1)}, bf16[4,96,768]{2,1,0:T(8,128)(2,1)S(1)}, u32[]{:S(2)}, u32[]{:S(2)}) collective-permute-start(bf16[4,96,768]{2,1,0:T(8,128)(2,1)S(1)} %get-tuple-element.96), channel_id=1, source_target_pairs={{0,2},{1,3},{2,0},{3,1},{4,6},{5,7},{6,4},{7,5},{8,10},{9,11},{10,... | collective-permute-start | bytes 1769480 | tf_op jit(solution)/shard_map/ppermute | solution.py:235
  104.7 25.7 %collective-permute-start.24 = (bf16[4,96,768]{2,1,0:T(8,128)(2,1)S(1)}, bf16[4,96,768]{2,1,0:T(8,128)(2,1)S(1)}, u32[]{:S(2)}, u32[]{:S(2)}) collective-permute-start(bf16[4,96,768]{2,1,0:T(8,128)(2,1)S(1)} %get-tuple-element.97), channel_id=1, source_target_pairs={{0,3},{1,2},{2,1},{3,0},{4,7},{5,6},{6,5},{7,4},{8,11},{9,10},{10,... | collective-permute-start | bytes 1769480 | tf_op jit(solution)/shard_map/ppermute | solution.py:235
  151.7 29.3 %collective-permute-start.31 = (bf16[4,96,768]{2,1,0:T(8,128)(2,1)S(1)}, bf16[4,96,768]{2,1,0:T(8,128)(2,1)S(1)}, u32[]{:S(2)}, u32[]{:S(2)}) collective-permute-start(bf16[4,96,768]{2,1,0:T(8,128)(2,1)S(1)} %pad_maximum_fusion.7.refs_0_), channel_id=1, source_target_pairs={{0,1},{1,0},{2,3},{3,2},{4,5},{5,4},{6,7},{7,6},{8,9},{9,8},{10,11... | collective-permute-start | bytes 1769480 | tf_op jit(solution)/shard_map/ppermute | solution.py:235
  153.3 37.5 %collective-permute-start.32 = (bf16[4,96,768]{2,1,0:T(8,128)(2,1)S(1)}, bf16[4,96,768]{2,1,0:T(8,128)(2,1)S(1)}, u32[]{:S(2)}, u32[]{:S(2)}) collective-permute-start(bf16[4,96,768]{2,1,0:T(8,128)(2,1)S(1)} %pad_maximum_fusion.7.refs_0_), channel_id=1, source_target_pairs={{0,2},{1,3},{2,0},{3,1},{4,6},{5,7},{6,4},{7,5},{8,10},{9,11},{10,... | collective-permute-start | bytes 1769480 | tf_op jit(solution)/shard_map/ppermute | solution.py:235
  159.9 32.8 %collective-permute-start.33 = (bf16[4,96,768]{2,1,0:T(8,128)(2,1)S(1)}, bf16[4,96,768]{2,1,0:T(8,128)(2,1)S(1)}, u32[]{:S(2)}, u32[]{:S(2)}) collective-permute-start(bf16[4,96,768]{2,1,0:T(8,128)(2,1)S(1)} %pad_maximum_fusion.7.refs_0_), channel_id=1, source_target_pairs={{0,3},{1,2},{2,1},{3,0},{4,7},{5,6},{6,5},{7,4},{8,11},{9,10},{10,... | collective-permute-start | bytes 1769480 | tf_op jit(solution)/shard_map/ppermute | solution.py:235
  215.8 34.8 %collective-permute-start.40 = (bf16[4,96,768]{2,1,0:T(8,128)(2,1)S(1)}, bf16[4,96,768]{2,1,0:T(8,128)(2,1)S(1)}, u32[]{:S(2)}, u32[]{:S(2)}) collective-permute-start(bf16[4,96,768]{2,1,0:T(8,128)(2,1)S(1)} %pad_maximum_fusion.8.refs_0_), channel_id=1, source_target_pairs={{0,1},{1,0},{2,3},{3,2},{4,5},{5,4},{6,7},{7,6},{8,9},{9,8},{10,11... | collective-permute-start | bytes 1769480 | tf_op jit(solution)/shard_map/ppermute | solution.py:235
  217.0 33.5 %collective-permute-start.41 = (bf16[4,96,768]{2,1,0:T(8,128)(2,1)S(1)}, bf16[4,96,768]{2,1,0:T(8,128)(2,1)}, u32[]{:S(2)}, u32[]{:S(2)}) collective-permute-start(bf16[4,96,768]{2,1,0:T(8,128)(2,1)S(1)} %pad_maximum_fusion.8.refs_0_), channel_id=1, source_target_pairs={{0,2},{1,3},{2,0},{3,1},{4,6},{5,7},{6,4},{7,5},{8,10},{9,11},{10,... | collective-permute-start | bytes 1769480 | tf_op jit(solution)/shard_map/ppermute | solution.py:235
  218.3 32.2 %collective-permute-start.42 = (bf16[4,96,768]{2,1,0:T(8,128)(2,1)S(1)}, bf16[4,96,768]{2,1,0:T(8,128)(2,1)}, u32[]{:S(2)}, u32[]{:S(2)}) collective-permute-start(bf16[4,96,768]{2,1,0:T(8,128)(2,1)S(1)} %pad_maximum_fusion.8.refs_0_), channel_id=1, source_target_pairs={{0,3},{1,2},{2,1},{3,0},{4,7},{5,6},{6,5},{7,4},{8,11},{9,10},{10,... | collective-permute-start | bytes 1769480 | tf_op jit(solution)/shard_map/ppermute | solution.py:235
  266.9 27.7 %collective-permute-start.51 = (bf16[4,96,768]{2,1,0:T(8,128)(2,1)}, bf16[4,96,768]{2,1,0:T(8,128)(2,1)}, u32[]{:S(2)}, u32[]{:S(2)}) collective-permute-start(bf16[4,96,768]{2,1,0:T(8,128)(2,1)} %get-tuple-element.108), channel_id=1, source_target_pairs={{0,3},{1,2},{2,1},{3,0},{4,7},{5,6},{6,5},{7,4},{8,11},{9,10},{10,... | collective-permute-start | bytes 1769480 | tf_op jit(solution)/shard_map/ppermute | solution.py:235
  284.7 26.3 %collective-permute-start.60 = (bf16[4,96,768]{2,1,0:T(8,128)(2,1)S(1)}, bf16[4,96,768]{2,1,0:T(8,128)(2,1)S(1)}, u32[]{:S(2)}, u32[]{:S(2)}) collective-permute-start(bf16[4,96,768]{2,1,0:T(8,128)(2,1)S(1)} %get-tuple-element.117), channel_id=1, source_target_pairs={{0,2},{1,3},{2,0},{3,1},{4,6},{5,7},{6,4},{7,5},{8,10},{9,11},{10,... | collective-permute-start | bytes 1769480 | tf_op jit(solution)/shard_map/ppermute | solution.py:235
  286.1 26.6 %collective-permute-start.61 = (bf16[4,96,768]{2,1,0:T(8,128)(2,1)S(1)}, bf16[4,96,768]{2,1,0:T(8,128)(2,1)S(1)}, u32[]{:S(2)}, u32[]{:S(2)}) collective-permute-start(bf16[4,96,768]{2,1,0:T(8,128)(2,1)S(1)} %get-tuple-element.118), channel_id=1, source_target_pairs={{0,3},{1,2},{2,1},{3,0},{4,7},{5,6},{6,5},{7,4},{8,11},{9,10},{10,... | collective-permute-start | bytes 1769480 | tf_op jit(solution)/shard_map/ppermute | solution.py:235
  445.7 93.5 %collective-permute-start.98 = (bf16[4,768,768]{2,1,0:T(8,128)(2,1)}, bf16[4,768,768]{2,1,0:T(8,128)(2,1)}, u32[]{:S(2)}, u32[]{:S(2)}) collective-permute-start(bf16[4,768,768]{2,1,0:T(8,128)(2,1)} %shard_map.257), channel_id=1, source_target_pairs={{0,16},{16,0},{1,17},{17,1},{2,18},{18,2},{3,19},{19,3},{4,20},{20... | collective-permute-start | bytes 14155784 | tf_op jit(solution)/shard_map/ppermute | solution.py:247
  464.3 83.8 %collective-permute-start.97 = (bf16[4,768,768]{2,1,0:T(8,128)(2,1)}, bf16[4,768,768]{2,1,0:T(8,128)(2,1)}, u32[]{:S(2)}, u32[]{:S(2)}) collective-permute-start(bf16[4,768,768]{2,1,0:T(8,128)(2,1)} %shard_map.255), channel_id=1, source_target_pairs={{0,16},{16,0},{1,17},{17,1},{2,18},{18,2},{3,19},{19,3},{4,20},{20... | collective-permute-start | bytes 14155784 | tf_op jit(solution)/shard_map/ppermute | solution.py:247
  506.1 24.4 %collective-permute-start.55 = (bf16[256,768]{1,0:T(8,128)(2,1)}, bf16[256,768]{1,0:T(8,128)(2,1)}, u32[]{:S(2)}, u32[]{:S(2)}) collective-permute-start(bf16[256,768]{1,0:T(8,128)(2,1)} %get-tuple-element.289), channel_id=1, source_target_pairs={{0,1},{1,0},{2,3},{3,2},{4,5},{5,4},{6,7},{7,6},{8,9},{9,8},{10,11... | collective-permute-start | bytes 1179656 | tf_op jit(solution)/shard_map/ppermute | solution.py:235
  507.2 24.4 %collective-permute-start.56 = (bf16[256,768]{1,0:T(8,128)(2,1)}, bf16[256,768]{1,0:T(8,128)(2,1)}, u32[]{:S(2)}, u32[]{:S(2)}) collective-permute-start(bf16[256,768]{1,0:T(8,128)(2,1)} %get-tuple-element.289), channel_id=1, source_target_pairs={{0,2},{1,3},{2,0},{3,1},{4,6},{5,7},{6,4},{7,5},{8,10},{9,11},{10,... | collective-permute-start | bytes 1179656 | tf_op jit(solution)/shard_map/ppermute | solution.py:235
  523.3 39.8 %all-to-all-start = ((bf16[4,200,785]{2,1,0:T(8,128)(2,1)}), bf16[4,200,785]{2,1,0:T(8,128)(2,1)}, u32[]{:S(2)}, u32[]{:S(2)}) async-start(bf16[4,200,785]{2,1,0:T(8,128)(2,1)} %pad_maximum_fusion.2), calls=%async_computation | async-start | bytes 2867200 | tf_op jit(solution)/shard_map/all_to_all | solution.py:251
  530.5 25.5 %collective-permute-start.94 = (bf16[256,768]{1,0:T(8,128)(2,1)}, bf16[256,768]{1,0:T(8,128)(2,1)S(1)}, u32[]{:S(2)}, u32[]{:S(2)}) collective-permute-start(bf16[256,768]{1,0:T(8,128)(2,1)} %get-tuple-element.280), channel_id=1, source_target_pairs={{0,1},{1,0},{2,3},{3,2},{4,5},{5,4},{6,7},{7,6},{8,9},{9,8},{10,11... | collective-permute-start | bytes 1179656 | tf_op jit(solution)/shard_map/ppermute | solution.py:235
  531.5 24.5 %collective-permute-start.95 = (bf16[256,768]{1,0:T(8,128)(2,1)}, bf16[256,768]{1,0:T(8,128)(2,1)S(1)}, u32[]{:S(2)}, u32[]{:S(2)}) collective-permute-start(bf16[256,768]{1,0:T(8,128)(2,1)} %get-tuple-element.279), channel_id=1, source_target_pairs={{0,2},{1,3},{2,0},{3,1},{4,6},{5,7},{6,4},{7,5},{8,10},{9,11},{10,... | collective-permute-start | bytes 1179656 | tf_op jit(solution)/shard_map/ppermute | solution.py:235
  539.2 53.7 %collective-permute-start.58 = (bf16[1024,768]{0,1:T(8,128)(2,1)}, bf16[1024,768]{0,1:T(8,128)(2,1)}, u32[]{:S(2)}, u32[]{:S(2)}) collective-permute-start(bf16[1024,768]{0,1:T(8,128)(2,1)} %get-tuple-element.274), channel_id=1, source_target_pairs={{0,16},{16,0},{1,17},{17,1},{2,18},{18,2},{3,19},{19,3},{4,20},{20... | collective-permute-start | bytes 4718600 | tf_op jit(solution)/shard_map/ppermute | solution.py:247
  585.9 28.1 %collective-permute-start.104 = (bf16[1024,768]{0,1:T(8,128)(2,1)}, bf16[1024,768]{0,1:T(8,128)(2,1)S(1)}, u32[]{:S(2)}, u32[]{:S(2)}) collective-permute-start(bf16[1024,768]{0,1:T(8,128)(2,1)} %get-tuple-element.272), channel_id=1, source_target_pairs={{0,16},{16,0},{1,17},{17,1},{2,18},{18,2},{3,19},{19,3},{4,20},{20... | collective-permute-start | bytes 4718600 | tf_op jit(solution)/shard_map/ppermute | solution.py:247
  (322 other events, 2953.7 us)
Sparse Core Ops, SparseCore 0:
  9.6 26.2 all-gather.2
  37.4 23.0 all-gather.4
